TPU v7x, 256 devices: a whole 4x4x8 slice. The times are simulated.
256 devices in a mesh: gz: 64 (over x, y, z_lo), gy: 4 (over z_hi, core).
Axes of the slice: x: 4, y: 4, z: 8 (z_hi: 2, z_lo: 4; z = z_hi * 4 + z_lo), core: 2. Of those that a mesh axis runs over, the one named last changes fastest.
Arguments:
- potential: float32 [192, 512, 2048], P('gz', 'gy'), may hold values from -3 to 301
- external: float32 [192, 512, 2048], P('gz', 'gy'), may hold values from -4 to 4
Outputs:
- dual_field: float32 [192, 512, 2048], P('gz', 'gy')
- density_log: float32 [192, 512, 2048], P('gz', 'gy')
All inputs are finite; a program needn't handle non-finite values.
Results may differ from a plain program's by a relative error of at most 0.0001.
Values sent between devices are 32-bit elements; how exact they have to be, the bound alone decides.
A program may use at most 128 MiB of HBM per device.

v0:
```python
import jax
import jax.numpy as jnp
from jax import lax
from jax.sharding import PartitionSpec as P

RADIUS = 128


HIGHEST = lax.Precision.HIGHEST


def padded_2(cells, sides, width):
    for axis, dim in sides:
        count = lax.axis_size(axis)
        ends = count - 1
        head = lax.slice_in_dim(cells, 0, width, axis=dim)
        tail = lax.slice_in_dim(cells, cells.shape[dim] - width, cells.shape[dim], axis=dim)
        cells = jnp.concatenate(
            [
                lax.ppermute(tail, axis, [(i, (i + 1) % count) for i in range(ends)]),
                cells,
                lax.ppermute(head, axis, [((i + 1) % count, i) for i in range(ends)]),
            ],
            axis=dim,
        )
    return cells


def log_kernel(row_count, col_count, offset, radius):
    in_index = lax.broadcasted_iota(jnp.int32, (row_count, col_count), 0)
    out_index = lax.broadcasted_iota(jnp.int32, (row_count, col_count), 1)
    apart = in_index - offset - out_index
    distance = apart.astype(jnp.float32)
    inside = jnp.abs(apart) <= radius
    return jnp.where(inside, jnp.exp(-2.0 * distance * distance / float(radius * radius)), 0.0)


def along_last(source, radius):
    leading = source.shape[:-1]
    length = source.shape[-1]
    block_size = 2 * radius
    block_count = length // block_size
    border = jnp.full(leading + (radius,), -jnp.inf, jnp.float32)
    padded = jnp.concatenate([border, source, border], axis=-1)
    pieces = padded.reshape(leading + (block_count + 1, block_size))
    window = jnp.concatenate([pieces[..., :-1, :], pieces[..., 1:, :]], axis=-1)
    highest_value = jnp.max(window, axis=-1, keepdims=True)
    weights = jnp.exp(window - highest_value)
    kernel_table = log_kernel(2 * block_size, block_size, radius, radius)
    summed = jnp.einsum("...w,wo->...o", weights, kernel_table, precision=HIGHEST)
    return (jnp.log(summed) + highest_value).reshape(leading + (length,))


def along_middle(extended, own_rows, radius):
    highest_value = jnp.max(extended, axis=1, keepdims=True)
    weights = jnp.exp(extended - highest_value)
    kernel_table = log_kernel(own_rows + 2 * radius, own_rows, radius, radius)
    summed = jnp.einsum("zwx,wo->zox", weights, kernel_table, precision=HIGHEST)
    return jnp.log(summed) + highest_value


def along_first(source, radius):
    length = source.shape[0]
    highest_value = jnp.max(source, axis=0, keepdims=True)
    weights = jnp.exp(source - highest_value)
    kernel_table = log_kernel(length, length, 0, radius)
    summed = jnp.einsum("wyx,wo->oyx", weights, kernel_table, precision=HIGHEST)
    return jnp.log(summed) + highest_value


def proximal(logs, outer_field):
    shifted = logs - 0.5 * outer_field
    softer = jnp.maximum(shifted, 0.0) + jnp.log1p(jnp.exp(-jnp.abs(shifted)))
    log_level = jnp.log1p(softer)
    for newton_step in range(2):
        exp_level = jnp.exp(log_level)
        log_level = log_level - (log_level + exp_level - shifted) / (1.0 + exp_level)
    return (log_level - logs, log_level)


def local(potential, external):
    depth = RADIUS
    position = lax.axis_index("gy")
    devices = lax.axis_size("gy")
    own_rows = potential.shape[1]
    row_index = lax.broadcasted_iota(jnp.int32, (1, own_rows + 2 * depth, 1), 1)
    outside = (row_index < depth) & (position == 0) | (row_index >= own_rows + depth) & (
        position == devices - 1
    )
    along_x = along_last(potential, depth)
    extended = padded_2(along_x, (("gy", 1),), depth)
    extended = jnp.where(outside, -jnp.inf, extended)
    along_y = along_middle(extended, own_rows, depth)
    pencil_logs, pencil_outer = (
        lax.all_to_all(along_y, "gz", split_axis=1, concat_axis=0, tiled=True),
        lax.all_to_all(external, "gz", split_axis=1, concat_axis=0, tiled=True),
    )
    along_z = along_first(pencil_logs, depth)
    dual_part, density_part = proximal(along_z, pencil_outer)
    slab_dual, slab_density = (
        lax.all_to_all(dual_part, "gz", split_axis=0, concat_axis=1, tiled=True),
        lax.all_to_all(density_part, "gz", split_axis=0, concat_axis=1, tiled=True),
    )
    return (slab_dual, slab_density)


def solution(mesh):
    return jax.shard_map(
        local,
        mesh=mesh,
        in_specs=(P("gz", "gy", None), P("gz", "gy", None)),
        out_specs=(P("gz", "gy", None), P("gz", "gy", None)),
        check_vma=False,
    )
```

profile of v0, /device:TPU:1, one launch (start us, length us, event | category | flops | bytes accessed | tf_op | source)
XLA Modules:
  0.0 470.3 jit_solution(14555783318927133353)
XLA Ops:
  0.6 6.0 %copy.39 = f32[3,128,2048]{2,0,1:T(4,128)} copy(f32[3,128,2048]{2,1,0:T(8,128)} %param.3) | data formatting | bytes 6291456 | tf_op args[1]
  6.6 12.8 %all-to-all-start.1 = ((f32[3,128,2048]{2,0,1:T(4,128)}), f32[3,128,2048]{2,0,1:T(4,128)}, u32[]{:S(2)}, u32[]{:S(2)}) async-start(f32[3,128,2048]{2,0,1:T(4,128)} %copy.39), calls=%async_computation.1 | async-start | bytes 8388608 | tf_op jit(solution)/shard_map/all_to_all | solution.py:96
  19.4 2.9 copy.32
  22.4 0.2 pad_maximum_fusion
  22.6 0.8 slice_reduce_fusion
  23.4 12.3 %log_add_fusion.1 = f32[3,128,8,256]{3,1,2,0:T(8,128)} fusion(f32[3,128,8,256]{1,3,2,0:T(8,128)S(1)} %get-tuple-element.8, f32[3,128,8,256]{1,3,2,0:T(8,128)S(1)} %get-tuple-element.9, f32[3,128,8]{1,2,0:T(8,128)S(1)} %reduce_max.40, s32[512]{0:T(512)S(1)} %iota_add_fusion), kind=kOutput, calls=%fused_computation.31 | convolution fusion | flops 4836818944 | bytes 9451520 | tf_op jit(solution)/shard_map/...w,wo->...o/dot_general | solution.py:50
  35.8 2.5 copy.34
  38.3 2.9 collective-permute-start.1
  41.2 6.6 %collective-permute-start = (f32[3,128,2048]{1,2,0:T(8,128)S(1)}, f32[3,128,2048]{1,2,0:T(8,128)}, u32[]{:S(2)}, u32[]{:S(2)}) collective-permute-start(f32[3,128,2048]{1,2,0:T(8,128)S(1)} %bitcast.38), channel_id=1, source_target_pairs={{0,1},{1,2},{2,3},{4,5},{5,6},{6,7},{8,9},{9,10},{10,11},{12,13},{... | collective-permute-start | bytes 9437192 | tf_op jit(solution)/shard_map/ppermute | solution.py:20
  47.8 111.6 %collective-permute-done.1 = f32[3,128,2048]{1,2,0:T(8,128)} collective-permute-done((f32[3,128,2048]{1,2,0:T(8,128)S(1)}, f32[3,128,2048]{1,2,0:T(8,128)}, u32[]{:S(2)}, u32[]{:S(2)}) %collective-permute-start.1) | collective-permute-done | bytes 3145760 | tf_op jit(solution)/shard_map/ppermute | solution.py:22
  159.4 0.0 collective-permute-done
  159.4 3.3 fusion.8
  162.7 13.1 %add_bitcast_fusion = f32[3,128,2048]{2,1,0:T(8,128)S(1)} fusion(f32[3,2048]{1,0:T(4,128)S(1)} %fusion.8, f32[3,128,2048]{1,2,0:T(8,128)} %collective-permute-done.1, f32[3,128,2048]{1,2,0:T(8,128)S(1)} %bitcast.40, f32[3,128,2048]{1,2,0:T(8,128)} %collective-permute-done, pred[384]{0:T(512)(128)(4,1)S(1)} %fusion.71, s32[384]{0:T(512)S(1)} %iota_add_fusion.1), kind=kOutput, calls=%fused_computation.30 | convolution fusion | flops 3634495488 | bytes 12609408 | tf_op jit(solution)/shard_map/zwx,wo->zox/dot_general | solution.py:58
  175.9 4.1 copy.36
  180.0 1.5 all-to-all-done.1
  181.5 9.2 %all-to-all-start = ((f32[3,128,2048]{2,0,1:T(4,128)}), f32[3,128,2048]{2,0,1:T(4,128)}, u32[]{:S(2)}, u32[]{:S(2)}) async-start(f32[3,128,2048]{2,0,1:T(4,128)} %copy.36), calls=%async_computation | async-start | bytes 8388608 | tf_op jit(solution)/shard_map/all_to_all | solution.py:95
  190.7 3.3 broadcast_multiply_fusion
  194.0 2.9 copy.40
  196.9 88.7 %all-to-all-done = f32[3,128,2048]{2,0,1:T(4,128)} async-done(((f32[3,128,2048]{2,0,1:T(4,128)}), f32[3,128,2048]{2,0,1:T(4,128)}, u32[]{:S(2)}, u32[]{:S(2)}) %all-to-all-start) | async-done | bytes 3145760 | tf_op jit(solution)/shard_map/all_to_all | solution.py:95
  285.6 5.4 %bitcast_reduce_fusion = (f32[2,2048]{1,0:T(2,128)S(1)}, f32[3,64,2,2048]{3,2,0,1:T(2,128)S(1)}) fusion(f32[3,64,2,2048]{3,0,2,1:T(4,128)} %bitcast.7), kind=kLoop, calls=%fused_computation.24 | loop fusion | flops 782336 | bytes 6307840 | tf_op jit(solution)/shard_map/reduce_max | solution.py:64
  291.0 11.1 %fusion.87 = (f32[192,2,2048]{2,0,1:T(8,128)S(1)}, f32[192,2,2048]{2,0,1:T(8,128)}) fusion(f32[192,2,2048]{2,1,0:T(2,128)S(1)} %bitcast.41, f32[2,2048]{1,0:T(2,128)S(1)} %get-tuple-element.6, f32[192,2,2048]{2,1,0:T(2,128)S(1)} %bitcast.42), kind=kOutput, calls=%fused_computation.100 | convolution fusion | flops 1826390016 | bytes 12599296 | tf_op jit(solution)/shard_map/wyx,wo->oyx/dot_general | solution.py:67
  302.1 4.1 copy.42
  306.2 6.0 %all-to-all-start.2 = ((f32[192,2,2048]{2,1,0:T(2,128)}), f32[192,2,2048]{2,1,0:T(2,128)S(1)}, u32[]{:S(2)}, u32[]{:S(2)}) async-start(f32[192,2,2048]{2,1,0:T(2,128)} %copy.42), calls=%async_computation.2 | async-start | bytes 6291456 | tf_op jit(solution)/shard_map/all_to_all | solution.py:101
  312.2 6.0 %copy.44 = f32[192,2,2048]{2,1,0:T(2,128)} copy(f32[192,2,2048]{2,0,1:T(8,128)} %get-tuple-element.5) | data formatting | bytes 6291456 | tf_op jit(solution)/shard_map/sub | solution.py:77
  318.2 66.7 %all-to-all-done.2 = f32[192,2,2048]{2,1,0:T(2,128)S(1)} async-done(((f32[192,2,2048]{2,1,0:T(2,128)}), f32[192,2,2048]{2,1,0:T(2,128)S(1)}, u32[]{:S(2)}, u32[]{:S(2)}) %all-to-all-start.2) | async-done | bytes 3145760 | tf_op jit(solution)/shard_map/all_to_all | solution.py:101
  384.8 5.8 %all-to-all-start.3 = ((f32[192,2,2048]{2,1,0:T(2,128)}), f32[192,2,2048]{2,1,0:T(2,128)}, u32[]{:S(2)}, u32[]{:S(2)}) async-start(f32[192,2,2048]{2,1,0:T(2,128)} %copy.44), calls=%async_computation.3 | async-start | bytes 6291456 | tf_op jit(solution)/shard_map/all_to_all | solution.py:102
  390.7 3.4 copy.43
  394.1 5.2 %all_to_all.54 = f32[3,128,2048]{2,1,0:T(8,128)} reshape(f32[3,64,2,2048]{3,2,1,0:T(2,128)} %copy.43) | data formatting | bytes 6291456 | tf_op jit(solution)/shard_map/all_to_all | solution.py:101
  399.4 63.6 %all-to-all-done.3 = f32[192,2,2048]{2,1,0:T(2,128)} async-done(((f32[192,2,2048]{2,1,0:T(2,128)}), f32[192,2,2048]{2,1,0:T(2,128)}, u32[]{:S(2)}, u32[]{:S(2)}) %all-to-all-start.3) | async-done | bytes 3145760 | tf_op jit(solution)/shard_map/all_to_all | solution.py:102
  463.0 3.7 copy.45
  466.7 3.4 all_to_all.58
  (5 shorter events, 0.0 us)
Async XLA Ops:
  6.6 174.9 %all-to-all-start.1 = ((f32[3,128,2048]{2,0,1:T(4,128)}), f32[3,128,2048]{2,0,1:T(4,128)}, u32[]{:S(2)}, u32[]{:S(2)}) async-start(f32[3,128,2048]{2,0,1:T(4,128)} %copy.39), calls=%async_computation.1 | async-start | bytes 8388608 | tf_op jit(solution)/shard_map/all_to_all | solution.py:96
  38.3 121.1 %collective-permute-start.1 = (f32[3,128,2048]{1,2,0:T(8,128)S(1)}, f32[3,128,2048]{1,2,0:T(8,128)}, u32[]{:S(2)}, u32[]{:S(2)}) collective-permute-start(f32[3,128,2048]{1,2,0:T(8,128)S(1)} %bitcast.37), channel_id=1, source_target_pairs={{1,0},{2,1},{3,2},{5,4},{6,5},{7,6},{9,8},{10,9},{11,10},{13,12},{... | collective-permute-start | bytes 9437192 | tf_op jit(solution)/shard_map/ppermute | solution.py:22
  41.2 118.2 %collective-permute-start = (f32[3,128,2048]{1,2,0:T(8,128)S(1)}, f32[3,128,2048]{1,2,0:T(8,128)}, u32[]{:S(2)}, u32[]{:S(2)}) collective-permute-start(f32[3,128,2048]{1,2,0:T(8,128)S(1)} %bitcast.38), channel_id=1, source_target_pairs={{0,1},{1,2},{2,3},{4,5},{5,6},{6,7},{8,9},{9,10},{10,11},{12,13},{... | collective-permute-start | bytes 9437192 | tf_op jit(solution)/shard_map/ppermute | solution.py:20
  181.5 104.1 %all-to-all-start = ((f32[3,128,2048]{2,0,1:T(4,128)}), f32[3,128,2048]{2,0,1:T(4,128)}, u32[]{:S(2)}, u32[]{:S(2)}) async-start(f32[3,128,2048]{2,0,1:T(4,128)} %copy.36), calls=%async_computation | async-start | bytes 8388608 | tf_op jit(solution)/shard_map/all_to_all | solution.py:95
  306.2 78.7 %all-to-all-start.2 = ((f32[192,2,2048]{2,1,0:T(2,128)}), f32[192,2,2048]{2,1,0:T(2,128)S(1)}, u32[]{:S(2)}, u32[]{:S(2)}) async-start(f32[192,2,2048]{2,1,0:T(2,128)} %copy.42), calls=%async_computation.2 | async-start | bytes 6291456 | tf_op jit(solution)/shard_map/all_to_all | solution.py:101
  384.8 78.2 %all-to-all-start.3 = ((f32[192,2,2048]{2,1,0:T(2,128)}), f32[192,2,2048]{2,1,0:T(2,128)}, u32[]{:S(2)}, u32[]{:S(2)}) async-start(f32[192,2,2048]{2,1,0:T(2,128)} %copy.44), calls=%async_computation.3 | async-start | bytes 6291456 | tf_op jit(solution)/shard_map/all_to_all | solution.py:102
where the time goes:
time: 474 us; the launch traced here: 470 us
  waiting for transfers between devices  332 us (70%)
  local copies, waits for them, and re-layouts  44.3 us (9%)
  starting transfers between devices  43.3 us (9%)
  matrix products  36.6 us (8%)
  other arithmetic  13 us (3%)
    ppermute x1, waiting for transfers between devices, padded_2(): lax.ppermute(head, axis, [((i + 1) % count, i) for i in range(ends)])  112 us
    all_to_all x1, waiting for transfers between devices, local(): lax.all_to_all(along_y, 'gz', split_axis=1, concat_axis=0, tiled=True)  88.7 us
    all_to_all x1, waiting for transfers between devices, local(): lax.all_to_all(dual_part, 'gz', split_axis=0, concat_axis=1, tiled=True)  66.7 us
    all_to_all x1, waiting for transfers between devices, local(): lax.all_to_all(density_part, 'gz', split_axis=0, concat_axis=1, tiled=True)  63.6 us
    dot_general x1, matrix products, along_middle(): summed = jnp.einsum('zwx,wo->zox', weights, kernel_table, precision=HIGHEST)  13.1 us
    all_to_all x1, starting transfers between devices, local(): lax.all_to_all(external, 'gz', split_axis=1, concat_axis=0, tiled=True)  12.8 us
    dot_general x1, matrix products, along_last(): jnp.einsum('...w,wo->...o', weights, kernel_table, precision=HIGHEST)  12.3 us
    dot_general x1, matrix products, along_first(): summed = jnp.einsum('wyx,wo->oyx', weights, kernel_table, precision=HIGHEST)  11.1 us
  transfers between devices with their start and end apart: 6, of which 5 were waited for; matrix products, arithmetic and copies ran while one was open for 12% of the time, Pallas kernels for 0%

commit v1 on v0

v1 whole, which is shorter than its diff:
```python
import jax
import jax.numpy as jnp
from jax import lax
from jax.experimental import pallas as pl
from jax.experimental.pallas import tpu as pltpu
from jax.sharding import PartitionSpec as P

RADIUS = 128
LANES = 128
ROWS = 8
WIDE = 256


def log_kernel(row_count, col_count, offset, radius):
    in_index = lax.broadcasted_iota(jnp.int32, (row_count, col_count), 0)
    out_index = lax.broadcasted_iota(jnp.int32, (row_count, col_count), 1)
    apart = in_index - offset - out_index
    distance = apart.astype(jnp.float32)
    inside = jnp.abs(apart) <= radius
    return jnp.where(inside, jnp.exp(-2.0 * distance * distance / float(radius * radius)), 0.0)


def halves(values):
    high = values.astype(jnp.bfloat16)
    low = (values - high.astype(jnp.float32)).astype(jnp.bfloat16)
    return high, low


def table_halves(table):
    high = lax.reduce_precision(table, 8, 7)
    return high.astype(jnp.bfloat16), (table - high).astype(jnp.bfloat16)


def table_rows(table):
    high, low = table_halves(table)
    return jnp.concatenate([high, high, low], axis=0)


def table_cols(table):
    high, low = table_halves(table)
    return jnp.concatenate([high, high, low], axis=1)


def dot(left, right):
    return jnp.dot(left, right, preferred_element_type=jnp.float32)


def x_kernel(source, table, out):
    blocks = source.shape[-1] // LANES
    for r in range(source.shape[0]):
        peaks, weights = [], []
        for k in range(blocks):
            cells = source[r, :, k * LANES:(k + 1) * LANES]
            peak = jnp.max(cells, axis=1, keepdims=True)
            peaks.append(peak)
            weights.append(jnp.exp(cells - peak))
        for k in range(blocks // 2):
            near = [j for j in range(2 * k - 1, 2 * k + 3) if 0 <= j < blocks]
            top = peaks[near[0]]
            for j in near[1:]:
                top = jnp.maximum(top, peaks[j])
            window = jnp.concatenate([weights[j] * jnp.exp(peaks[j] - top) for j in near], axis=1)
            high, low = halves(window)
            start = (near[0] - (2 * k - 1)) * LANES
            width = len(near) * LANES
            size = 4 * LANES
            tall = [table[i * size + start:i * size + start + width, :] for i in range(3)]
            summed = dot(high, tall[0]) + dot(low, tall[1]) + dot(high, tall[2])
            logs = jnp.log(summed) + top
            turned = logs.T
            out[k * (WIDE // ROWS):(k + 1) * (WIDE // ROWS), r * ROWS:(r + 1) * ROWS, :] = turned.reshape(
                WIDE // ROWS, ROWS, LANES
            )


def yz_kernel(source, y_table, z_table, out, middle):
    groups, parts, rows, _ = source.shape
    depth = groups * rows // ROWS
    batch = 8
    size = 3 * LANES

    @pl.loop(0, groups // batch)
    def _(step):
        first = step * batch
        peaks, weights = [], []
        for b in range(parts):
            cells = source[pl.ds(first, batch), b].reshape(batch * rows, LANES)
            peak = jnp.max(cells, axis=1, keepdims=True)
            peaks.append(peak)
            weights.append(jnp.exp(cells - peak))
        for b in range(parts):
            near = [j for j in range(b - 1, b + 2) if 0 <= j < parts]
            top = peaks[near[0]]
            for j in near[1:]:
                top = jnp.maximum(top, peaks[j])
            window = jnp.concatenate([weights[j] * jnp.exp(peaks[j] - top) for j in near], axis=1)
            high, low = halves(window)
            start = (near[0] - (b - 1)) * LANES
            width = len(near) * LANES
            tall = [y_table[i * size + start:i * size + start + width, :] for i in range(3)]
            summed = dot(high, tall[0]) + dot(low, tall[1]) + dot(high, tall[2])
            at = pl.multiple_of(first * rows, batch * rows)
            middle[b, pl.ds(at, batch * rows), :] = jnp.log(summed) + top

    for b in range(parts):
        tops = jnp.max(middle[b].reshape(depth, ROWS, LANES), axis=0)
        for x in range(ROWS):
            cells = middle[b, pl.ds(x, depth, stride=ROWS), :]
            top = tops[x:x + 1, :]
            weights = jnp.exp(cells - top)
            high, low = halves(weights)
            summed = dot(z_table[...], jnp.concatenate([high, low, high], axis=0))
            middle[b, pl.ds(x, depth, stride=ROWS), :] = jnp.log(summed) + top
        out[:, b] = middle[b].reshape(groups, rows, LANES)


def proximal(logs, outer_field):
    shifted = logs - 0.5 * outer_field
    softer = jnp.maximum(shifted, 0.0) + jnp.log1p(jnp.exp(-jnp.abs(shifted)))
    log_level = jnp.log1p(softer)
    for newton_step in range(2):
        exp_level = jnp.exp(log_level)
        log_level = log_level - (log_level + exp_level - shifted) / (1.0 + exp_level)
    return log_level - logs, log_level


def end_kernel(source, outer, dual, density):
    blocks = outer.shape[-1] // WIDE
    per = WIDE // ROWS
    for r in range(outer.shape[0]):
        for k in range(blocks):
            turned = source[k * per:(k + 1) * per, r * ROWS:(r + 1) * ROWS, :].reshape(WIDE, LANES)
            at = slice(k * WIDE, (k + 1) * WIDE)
            dual_part, density_part = proximal(turned.T, outer[r, :, at])
            dual[r, :, at] = dual_part
            density[r, :, at] = density_part


PARAMS = pltpu.CompilerParams(vmem_limit_bytes=56 << 20)


def local(potential, external):
    depth, own_rows, length = potential.shape
    groups, parts = lax.axis_size("gz"), lax.axis_size("gy")
    devices = groups * parts
    rows = depth * ROWS
    vmem = pl.BlockSpec(memory_space=pltpu.VMEM)
    x_table = table_rows(log_kernel(4 * LANES, WIDE, RADIUS, RADIUS))
    y_table = table_rows(log_kernel(3 * LANES, LANES, RADIUS, RADIUS))
    z_table = table_cols(log_kernel(groups * depth, groups * depth, 0, RADIUS))
    tiles = jax.ShapeDtypeStruct((devices, rows, LANES), jnp.float32)
    along_x = pl.pallas_call(
        x_kernel, out_shape=tiles, in_specs=[vmem, vmem], out_specs=vmem, compiler_params=PARAMS, name="along_x"
    )(potential, x_table)
    received = lax.all_to_all(along_x, ("gz", "gy"), 0, 0, tiled=True)
    along_z = pl.pallas_call(
        yz_kernel,
        out_shape=jax.ShapeDtypeStruct((groups, parts, rows, LANES), jnp.float32),
        in_specs=[vmem] * 3,
        out_specs=vmem,
        scratch_shapes=[pltpu.VMEM((parts, groups * rows, LANES), jnp.float32)],
        compiler_params=PARAMS,
        name="along_yz",
    )(received.reshape(groups, parts, rows, LANES), y_table, z_table)
    returned = lax.all_to_all(along_z.reshape(devices, rows, LANES), ("gz", "gy"), 0, 0, tiled=True)
    field = jax.ShapeDtypeStruct(potential.shape, jnp.float32)
    return pl.pallas_call(
        end_kernel, out_shape=(field, field), in_specs=[vmem] * 2, out_specs=(vmem, vmem), compiler_params=PARAMS, name="proximal"
    )(returned, external)


def solution(mesh):
    return jax.shard_map(
        local,
        mesh=mesh,
        in_specs=(P("gz", "gy", None), P("gz", "gy", None)),
        out_specs=(P("gz", "gy", None), P("gz", "gy", None)),
        check_vma=False,
    )
```

time: 474 us -> 209 us (0.44)
  waiting for transfers between devices: 332 us -> 73.9 us
  blocking collectives: 0 us -> 84.6 us
  local copies, waits for them, and re-layouts: 44.3 us -> 1.66 us
  matrix products: 36.6 us -> 0 us
  Pallas kernels: 0 us -> 29.4 us
  starting transfers between devices: 43.3 us -> 15.6 us
  other arithmetic: 13 us -> 3.08 us
    all_to_all x4 -> x1, waiting for transfers between devices: 221 us -> 73.9 us  [local(): received = lax.all_to_all(along_x, ('gz', 'gy'), 0, 0, tiled=True)]
    ppermute x2 -> x0, waiting for transfers between devices: 112 us -> none  [the longest x1 112 us: padded_2(): lax.ppermute(head, axis, [((i + 1) % count, i) for i in range(ends)])]
    all_to_all x0 -> x1, blocking collectives: none -> 84.6 us  [local(): lax.all_to_all(along_z.reshape(devices, rows, LANES), ('gz', 'gy'), 0, 0,...]
    dot_general x3 -> x0, matrix products: 36.6 us -> none  [the longest x1 13.1 us: along_middle(): summed = jnp.einsum('zwx,wo->zox', weights, kernel_table, precision=HIGHEST)]
    pallas_call x0 -> x3, Pallas kernels: none -> 29.4 us  [the longest x1 12.4 us: local(): pl.pallas_call(yz_kernel, out_shape=jax.ShapeDtypeStruct((groups, parts,...]
    all_to_all x4 -> x1, starting transfers between devices: 33.8 us -> 15.6 us  [local(): received = lax.all_to_all(along_x, ('gz', 'gy'), 0, 0, tiled=True)]
    all_to_all x4 -> x0, local copies, waits for them, and re-layouts: 15.7 us -> none  [the longest x2 8.68 us: local(): lax.all_to_all(dual_part, 'gz', split_axis=0, concat_axis=1, tiled=True)]
    sub x2 -> x0, local copies, waits for them, and re-layouts: 10.1 us -> none  [the longest x1 6 us: proximal(): log_level - (log_level + exp_level - shifted) / (1.0 + exp_level)]
  transfers between devices with their start and end apart: 6 -> 1, of which waited for: 5 -> 1; matrix products, arithmetic and copies ran while one was open for 12% -> 1% of each run, Pallas kernels for 0% -> 0%
where the time goes in v1:
time: 209 us
  blocking collectives  84.6 us (40%)
  waiting for transfers between devices  73.9 us (35%)
  Pallas kernels  29.4 us (14%)
  starting transfers between devices  15.6 us (7%)
  other arithmetic  3.08 us (1%)
    all_to_all x1, blocking collectives, local(): lax.all_to_all(along_z.reshape(devices, rows, LANES), ('gz', 'gy'), 0, 0,...  84.6 us
    all_to_all x1, waiting for transfers between devices, local(): received = lax.all_to_all(along_x, ('gz', 'gy'), 0, 0, tiled=True)  73.9 us
    all_to_all x1, starting transfers between devices, local(): received = lax.all_to_all(along_x, ('gz', 'gy'), 0, 0, tiled=True)  15.6 us
    pallas_call x1, Pallas kernels, local(): pl.pallas_call(yz_kernel, out_shape=jax.ShapeDtypeStruct((groups, parts,...  12.4 us
    pallas_call x1, Pallas kernels, local(): pl.pallas_call(end_kernel, out_shape=(field, field), in_specs=[vmem] * 2,...  10 us
    pallas_call x1, Pallas kernels, local(): pl.pallas_call(x_kernel, out_shape=tiles, in_specs=[vmem, vmem], out_spec...  7.02 us
  transfers between devices with their start and end apart: 1, of which 1 were waited for; matrix products, arithmetic and copies ran while one was open for 1% of the time, Pallas kernels for 0%

profile of v1, /device:TPU:1, one launch (start us, length us, event | category | flops | bytes accessed | tf_op | source)
XLA Modules:
  0.0 209.0 jit_solution(12537844711402116270)
XLA Ops:
  0.6 0.3 reduce-precision_convert_fusion
  1.0 0.9 pad_maximum_fusion.table
  1.9 7.0 %along_x.1 = f32[256,24,128]{2,1,0:T(8,128)} custom-call(f32[3,128,2048]{2,1,0:T(8,128)} %source.1, bf16[1536,256]{1,0:T(8,128)(2,1)} %pad_maximum_fusion.table), custom_call_target="tpu_custom_call" | custom-call | tf_op jit(solution)/shard_map/along_x/pallas_call | solution.py:152
  8.9 15.6 %all-to-all-start = ((f32[256,24,128]{2,1,0:T(8,128)}), f32[256,24,128]{2,1,0:T(8,128)S(1)}, u32[]{:S(2)}, u32[]{:S(2)}) async-start(f32[256,24,128]{2,1,0:T(8,128)} %along_x.1), calls=%async_computation | async-start | bytes 6291456 | tf_op jit(solution)/shard_map/all_to_all | solution.py:155
  24.6 0.1 reduce-precision_convert_fusion.1
  24.7 0.8 pad_maximum_fusion.2.z_table
  25.5 0.2 reduce-precision_convert_fusion.2
  25.7 0.7 pad_maximum_fusion.1.y_table
  26.4 73.9 %all-to-all-done = f32[256,24,128]{2,1,0:T(8,128)S(1)} async-done(((f32[256,24,128]{2,1,0:T(8,128)}), f32[256,24,128]{2,1,0:T(8,128)S(1)}, u32[]{:S(2)}, u32[]{:S(2)}) %all-to-all-start) | async-done | bytes 3145760 | tf_op jit(solution)/shard_map/all_to_all | solution.py:155
  100.3 0.0 copy-start
  100.3 1.7 copy-done
  102.0 12.4 %along_yz.1 = f32[64,4,24,128]{3,2,1,0:T(8,128)} custom-call(f32[64,4,24,128]{3,2,1,0:T(8,128)} %bitcast.2, bf16[1152,128]{1,0:T(8,128)(2,1)} %pad_maximum_fusion.1.y_table, bf16[192,576]{1,0:T(8,128)(2,1)} %pad_maximum_fusion.2.z_table), custom_call_target="tpu_custom_call" | custom-call | tf_op jit(solution)/shard_map/along_yz/pallas_call | solution.py:156
  114.4 84.6 %all_to_all.10.source = f32[256,24,128]{2,1,0:T(8,128)} all-to-all(f32[256,24,128]{2,1,0:T(8,128)} %bitcast.3), channel_id=1, replica_groups=mesh['gz'=64,'gy'=4] {'gz','gy'}, dimensions={0} | all-to-all | bytes 6291456 | tf_op jit(solution)/shard_map/all_to_all | solution.py:165
  199.0 10.0 %proximal.1 = (f32[3,128,2048]{2,1,0:T(8,128)}, f32[3,128,2048]{2,1,0:T(8,128)}) custom-call(f32[256,24,128]{2,1,0:T(8,128)} %all_to_all.10.source, f32[3,128,2048]{2,1,0:T(8,128)} %outer.1), custom_call_target="tpu_custom_call" | custom-call | tf_op jit(solution)/shard_map/proximal/pallas_call | solution.py:167
  (2 shorter events, 0.0 us)
Async XLA Ops:
  8.9 91.4 %all-to-all-start = ((f32[256,24,128]{2,1,0:T(8,128)}), f32[256,24,128]{2,1,0:T(8,128)S(1)}, u32[]{:S(2)}, u32[]{:S(2)}) async-start(f32[256,24,128]{2,1,0:T(8,128)} %along_x.1), calls=%async_computation | async-start | bytes 6291456 | tf_op jit(solution)/shard_map/all_to_all | solution.py:155
  100.3 1.7 copy-start

commit v2 on v1

v2 whole, which is shorter than its diff:
```python
import jax
import jax.numpy as jnp
from jax import lax
from jax.experimental import pallas as pl
from jax.experimental.pallas import tpu as pltpu
from jax.sharding import PartitionSpec as P

RADIUS = 128
LANES = 128
ROWS = 8
WIDE = 256


def log_kernel(row_count, col_count, offset, radius):
    in_index = lax.broadcasted_iota(jnp.int32, (row_count, col_count), 0)
    out_index = lax.broadcasted_iota(jnp.int32, (row_count, col_count), 1)
    apart = in_index - offset - out_index
    distance = apart.astype(jnp.float32)
    inside = jnp.abs(apart) <= radius
    return jnp.where(inside, jnp.exp(-2.0 * distance * distance / float(radius * radius)), 0.0)


def halves(values):
    high = values.astype(jnp.bfloat16)
    low = (values - high.astype(jnp.float32)).astype(jnp.bfloat16)
    return high, low


def table_halves(table):
    high = lax.reduce_precision(table, 8, 7)
    return high.astype(jnp.bfloat16), (table - high).astype(jnp.bfloat16)


def table_rows(table):
    high, low = table_halves(table)
    return jnp.concatenate([high, high, low], axis=0)


def table_cols(table):
    high, low = table_halves(table)
    return jnp.concatenate([high, high, low], axis=1)


def dot(left, right):
    return jnp.dot(left, right, preferred_element_type=jnp.float32)


MESH = pl.DeviceIdType.MESH
CHUNKS = 4
RING = 16
GROUPS = 4
EMPTY = -1e30


def chain_kernel(potential, x_table, y_table, z_table, home, cells, a, b, c, d, e, f, load_sem, send_sem, recv_sem, own_sem):
    depth, own_rows, length = potential.shape
    slab, part = lax.axis_index("gz"), lax.axis_index("gy")
    spot, lane = slab // GROUPS, slab % GROUPS
    core = part % 2
    level = (part // 2) * 4 + lane
    sign = 1 - 2 * core
    step_x = length // CHUNKS
    tile = a.shape[2]

    load = pltpu.make_async_copy(potential, cells.at[:, :, pl.ds(LANES, length)], load_sem)
    load.start()

    def z_peer(s):
        t = (s * 3) % RING
        to_level = (level + sign * (t % 8) + 8) % 8
        to_core = (core + t // 8) % 2
        return spot * GROUPS + to_level % 4, (to_level // 4) * 2 + to_core

    def xy_peer(s):
        t = (s * 5) % RING
        to_x = (spot // 4 + sign * (t % 4) + 4) % 4
        to_y = (spot % 4 + sign * (t // 4) + 4) % 4
        return to_x * 4 + to_y

    barrier = pltpu.get_barrier_semaphore()

    @pl.loop(1, RING)
    def _(s):
        pl.semaphore_signal(barrier, inc=1, device_id=z_peer(s), device_id_type=MESH)
        pl.semaphore_signal(barrier, inc=1, device_id=(xy_peer(s) * GROUPS + lane, part), device_id_type=MESH)

    def order(slab_of, part_of):
        return ((part_of // 2) * 4 + slab_of % GROUPS) * 2 + part_of % 2

    mine = order(slab, part)
    slot = lane * GROUPS + part

    def send(source, target, stage, chunk, device):
        pltpu.make_async_remote_copy(
            src_ref=source,
            dst_ref=target,
            send_sem=send_sem.at[stage, chunk],
            recv_sem=recv_sem.at[stage, chunk],
            device_id=device,
            device_id_type=MESH,
        ).start()

    def keep(source, target, stage, chunk):
        return pltpu.make_async_copy(source, target, own_sem.at[stage, chunk])

    def x_stage(chunk):
        @pl.loop(0, depth)
        def _(r):
            peaks, weights = [], []
            for k in range(6):
                at = pl.multiple_of(chunk * step_x + k * LANES, LANES)
                block = cells[r, :, pl.ds(at, LANES)]
                peak = jnp.max(block, axis=1, keepdims=True)
                peaks.append(peak)
                weights.append(jnp.exp(block - peak))
            size = 4 * LANES
            for k in range(2):
                near = range(2 * k, 2 * k + 4)
                top = peaks[near[0]]
                for j in near[1:]:
                    top = jnp.maximum(top, peaks[j])
                window = jnp.concatenate([weights[j] * jnp.exp(peaks[j] - top) for j in near], axis=1)
                high, low = halves(window)
                summed = (
                    dot(high, x_table[:size, :]) + dot(low, x_table[size:2 * size, :]) + dot(high, x_table[2 * size:, :])
                )
                turned = (jnp.log(summed) + top).T
                a[chunk, 8 * k:8 * k + 8, pl.ds(pl.multiple_of(r * 32, 32), 32), :] = turned.reshape(8, 32, LANES)

        return None

    def x_send(chunk):
        keep(a.at[chunk, mine], b.at[chunk, slot], 0, chunk).start()

        @pl.loop(1, RING)
        def _(s):
            to = z_peer(s)
            send(a.at[chunk, order(*to)], b.at[chunk, slot], 0, chunk, to)

    def arrive(stage, chunk, source, target):
        view = pltpu.make_async_remote_copy(
            src_ref=source,
            dst_ref=target,
            send_sem=send_sem.at[stage, chunk],
            recv_sem=recv_sem.at[stage, chunk],
            device_id=(slab, part),
            device_id_type=MESH,
        )
        return view

    def y_stage(chunk):
        keep(a.at[chunk, mine], b.at[chunk, slot], 0, chunk).wait()
        arrive(0, chunk, a.at[chunk, pl.ds(0, RING - 1)], b.at[chunk, pl.ds(0, RING - 1)]).wait_recv()
        size = 3 * LANES

        @pl.loop(0, GROUPS)
        def _(lo):
            peaks, weights = [], []
            for k in range(GROUPS):
                block = b[chunk, lo * GROUPS + k]
                peak = jnp.max(block, axis=1, keepdims=True)
                peaks.append(peak)
                weights.append(jnp.exp(block - peak))
            for k in range(GROUPS):
                near = [j for j in range(k - 1, k + 2) if 0 <= j < GROUPS]
                top = peaks[near[0]]
                for j in near[1:]:
                    top = jnp.maximum(top, peaks[j])
                window = jnp.concatenate([weights[j] * jnp.exp(peaks[j] - top) for j in near], axis=1)
                high, low = halves(window)
                start = (near[0] - (k - 1)) * LANES
                width = len(near) * LANES
                tall = [y_table[i * size + start:i * size + start + width, :] for i in range(3)]
                logs = jnp.log(dot(high, tall[0]) + dot(low, tall[1]) + dot(high, tall[2])) + top
                for r in range(depth):
                    for g in range(4):
                        at = pl.multiple_of((lo * depth + r) * ROWS, ROWS)
                        first = (r * 4 + g) * ROWS
                        c[chunk, k * 4 + g, pl.ds(at, ROWS), :] = logs[first:first + ROWS, :]

        rows = pl.ds(pl.multiple_of(spot * tile, tile), tile)
        keep(c.at[chunk, spot], d.at[chunk, rows], 1, chunk).start()

        @pl.loop(1, RING)
        def _(s):
            to = xy_peer(s)
            send(c.at[chunk, to], d.at[chunk, rows], 1, chunk, (to * GROUPS + lane, part))

    def z_stage(chunk):
        rows = pl.ds(pl.multiple_of(spot * tile, tile), tile)
        keep(c.at[chunk, spot], d.at[chunk, rows], 1, chunk).wait()
        arrive(1, chunk, c.at[chunk, pl.ds(0, RING - 1)], d.at[chunk, pl.ds(0, (RING - 1) * tile)]).wait_recv()
        deep = RING * tile // ROWS
        tops = jnp.max(d[chunk].reshape(deep, ROWS, LANES), axis=0)
        for x in range(0, ROWS, 2):
            top = jnp.concatenate([tops[x:x + 1, :], tops[x + 1:x + 2, :]], axis=1)
            pair = jnp.concatenate([d[chunk, pl.ds(x + i, deep, stride=ROWS), :] for i in range(2)], axis=1)
            high, low = halves(jnp.exp(pair - top))
            logs = jnp.log(dot(z_table[...], jnp.concatenate([high, low, high], axis=0))) + top
            for i in range(2):
                e[chunk, pl.ds(x + i, deep, stride=ROWS), :] = logs[:, i * LANES:(i + 1) * LANES]
        keep(e.at[chunk, rows], f.at[chunk, spot], 2, chunk).start()

        @pl.loop(1, RING)
        def _(s):
            to = xy_peer(s)
            there = pl.ds(pl.multiple_of(to * tile, tile), tile)
            send(e.at[chunk, there], f.at[chunk, spot], 2, chunk, (to * GROUPS + lane, part))

    def piece(chunk, slab_of, part_of):
        rows = tile // GROUPS
        at = pl.multiple_of((slab_of % GROUPS) * rows, rows)
        return f.at[chunk, pl.ds(part_of * 4, 4), pl.ds(at, rows)]

    def back_stage(chunk):
        rows = pl.ds(pl.multiple_of(spot * tile, tile), tile)
        keep(e.at[chunk, rows], f.at[chunk, spot], 2, chunk).wait()
        arrive(2, chunk, e.at[chunk, pl.ds(0, (RING - 1) * tile)], f.at[chunk, pl.ds(0, RING - 1)]).wait_recv()
        keep(piece(chunk, slab, part), home.at[chunk, mine], 3, chunk).start()

        @pl.loop(1, RING)
        def _(s):
            to = z_peer(s)
            send(piece(chunk, *to), home.at[chunk, mine], 3, chunk, to)

    edge = jnp.full((depth, own_rows, LANES), EMPTY, jnp.float32)
    cells[:, :, :LANES] = edge
    cells[:, :, LANES + length:] = edge
    load.wait()
    x_stage(0)
    pl.semaphore_wait(barrier, 2 * (RING - 1))
    x_send(0)

    @pl.loop(1, CHUNKS)
    def _(chunk):
        x_stage(chunk)
        x_send(chunk)

    @pl.loop(0, CHUNKS)
    def _(chunk):
        y_stage(chunk)

        @pl.when(chunk > 0)
        def _():
            back_stage(chunk - 1)

        z_stage(chunk)

    back_stage(CHUNKS - 1)

    @pl.loop(0, CHUNKS)
    def _(chunk):
        some = pl.ds(0, RING - 1)
        flat = pl.ds(0, (RING - 1) * tile)
        arrive(0, chunk, a.at[chunk, some], b.at[chunk, some]).wait_send()
        arrive(1, chunk, c.at[chunk, some], d.at[chunk, flat]).wait_send()
        arrive(2, chunk, e.at[chunk, flat], f.at[chunk, some]).wait_send()
        keep(piece(chunk, slab, part), home.at[chunk, mine], 3, chunk).wait()
        last = arrive(3, chunk, home.at[chunk, some], home.at[chunk, some])
        last.wait_send()
        last.wait_recv()


def proximal(logs, outer_field):
    shifted = logs - 0.5 * outer_field
    softer = jnp.maximum(shifted, 0.0) + jnp.log1p(jnp.exp(-jnp.abs(shifted)))
    log_level = jnp.log1p(softer)
    for newton_step in range(2):
        exp_level = jnp.exp(log_level)
        log_level = log_level - (log_level + exp_level - shifted) / (1.0 + exp_level)
    return log_level - logs, log_level


def end_kernel(source, outer, dual, density):
    blocks = outer.shape[-1] // WIDE
    per = WIDE // ROWS
    for k in range(blocks):
        turned = source[k * per:(k + 1) * per].reshape(WIDE, LANES)
        at = slice(k * WIDE, (k + 1) * WIDE)
        dual_part, density_part = proximal(turned.T, outer[0, :, at])
        dual[0, :, at] = dual_part
        density[0, :, at] = density_part


def local(potential, external):
    depth, own_rows, length = potential.shape
    groups = lax.axis_size("gz")
    rows = depth * ROWS
    tile = GROUPS * rows
    vmem = pl.BlockSpec(memory_space=pltpu.VMEM)
    anywhere = pl.BlockSpec(memory_space=pl.ANY)
    x_table = table_rows(log_kernel(4 * LANES, WIDE, RADIUS, RADIUS))
    y_table = table_rows(log_kernel(3 * LANES, LANES, RADIUS, RADIUS))
    z_table = table_cols(log_kernel(groups * depth, groups * depth, 0, RADIUS))
    stack = pltpu.VMEM((CHUNKS, RING, tile, LANES), jnp.float32)
    long = pltpu.VMEM((CHUNKS, RING * tile, LANES), jnp.float32)
    along_z = pl.pallas_call(
        chain_kernel,
        out_shape=jax.ShapeDtypeStruct((CHUNKS, RING, GROUPS, rows, LANES), jnp.float32),
        in_specs=[anywhere, vmem, vmem, vmem],
        out_specs=anywhere,
        scratch_shapes=[
            pltpu.VMEM((depth, own_rows, length + 2 * LANES), jnp.float32),
            stack,
            stack,
            stack,
            long,
            long,
            stack,
            pltpu.SemaphoreType.DMA,
            pltpu.SemaphoreType.DMA((4, CHUNKS)),
            pltpu.SemaphoreType.DMA((4, CHUNKS)),
            pltpu.SemaphoreType.DMA((4, CHUNKS)),
        ],
        compiler_params=pltpu.CompilerParams(collective_id=0, has_side_effects=True, vmem_limit_bytes=48 << 20),
        name="along_xyz",
    )(potential, x_table, y_table, z_table)
    field = jax.ShapeDtypeStruct(potential.shape, jnp.float32)
    wide = length // CHUNKS
    block = pl.BlockSpec((1, own_rows, wide), lambda r, k: (r, 0, k))
    return pl.pallas_call(
        end_kernel,
        grid=(depth, CHUNKS),
        out_shape=(field, field),
        in_specs=[pl.BlockSpec((wide // ROWS, ROWS, LANES), lambda r, k: (k, r, 0)), block],
        out_specs=(block, block),
        name="proximal",
    )(along_z.reshape(length // ROWS, rows, LANES), external)


def solution(mesh):
    return jax.shard_map(
        local,
        mesh=mesh,
        in_specs=(P("gz", "gy", None), P("gz", "gy", None)),
        out_specs=(P("gz", "gy", None), P("gz", "gy", None)),
        check_vma=False,
    )
```

time: 209 us -> 164 us (0.78)
  Pallas kernels: 29.4 us -> 161 us
  blocking collectives: 84.6 us -> 0 us
  waiting for transfers between devices: 73.9 us -> 0 us
  starting transfers between devices: 15.6 us -> 0 us
  other arithmetic: 3.08 us -> 0.8 us
    pallas_call x3 -> x2, Pallas kernels: 29.4 us -> 161 us  [the longest x1 149 us: local(): pl.pallas_call(chain_kernel, out_shape=jax.ShapeDtypeStruct((CHUNKS, RING...]
    all_to_all x1 -> x0, blocking collectives: 84.6 us -> none  [local(): lax.all_to_all(along_z.reshape(devices, rows, LANES), ('gz', 'gy'), 0, 0,...]
    all_to_all x1 -> x0, waiting for transfers between devices: 73.9 us -> none  [local(): received = lax.all_to_all(along_x, ('gz', 'gy'), 0, 0, tiled=True)]
    all_to_all x1 -> x0, starting transfers between devices: 15.6 us -> none  [local(): received = lax.all_to_all(along_x, ('gz', 'gy'), 0, 0, tiled=True)]
  transfers between devices with their start and end apart: 1 -> 0, of which waited for: 1 -> 0; matrix products, arithmetic and copies ran while one was open for 1% -> 0% of each run, Pallas kernels for 0% -> 0%
where the time goes in v2:
time: 164 us
  Pallas kernels  161 us (98%)
    pallas_call x1, Pallas kernels, local(): pl.pallas_call(chain_kernel, out_shape=jax.ShapeDtypeStruct((CHUNKS, RING...  149 us
    pallas_call x1, Pallas kernels, local(): pl.pallas_call(end_kernel, grid=(depth, CHUNKS), out_shape=(field, field)...  11.5 us

profile of v2, /device:TPU:1, one launch (start us, length us, event | category | flops | bytes accessed | tf_op | source)
XLA Modules:
  0.0 163.9 jit_solution(14112837812874332574)
XLA Ops:
  0.6 0.2 reduce-precision_convert_fusion.2
  0.9 0.1 reduce-precision_convert_fusion.1
  1.0 0.1 pad_maximum_fusion.2.z_table
  1.1 0.3 reduce-precision_convert_fusion
  1.4 0.1 pad_maximum_fusion.x_table
  1.5 149.2 %along_xyz.1 = f32[4,16,4,24,128]{4,3,2,1,0:T(8,128)S(1)} custom-call(f32[3,128,2048]{2,1,0:T(8,128)} %potential.1, bf16[1536,256]{1,0:T(8,128)(2,1)S(1)} %pad_maximum_fusion.x_table, bf16[1152,128]{1,0:T(8,128)(2,1)S(1)} %pad_maximum_fusion.1.y_table, bf16[192,576]{1,0:T(8,128)(2,1)S(1)} %pad_maximum_fusion.2.z_table), custom_call_target="tpu_custom_call" | custom-call | tf_op jit(solution)/shard_map/along_xyz/pallas_call | solution.py:297
  150.7 0.0 copy-start
  150.7 1.6 copy-done
  152.3 11.5 %proximal.1 = (f32[3,128,2048]{2,1,0:T(8,128)}, f32[3,128,2048]{2,1,0:T(8,128)}) custom-call(f32[256,24,128]{2,1,0:T(8,128)} %bitcast.1, f32[3,128,2048]{2,1,0:T(8,128)} %outer.1), custom_call_target="tpu_custom_call" | custom-call | tf_op jit(solution)/shard_map/proximal/pallas_call | solution.py:321
  (3 shorter events, 0.0 us)
Async XLA Ops:
  150.7 1.6 %copy-start = (f32[4,16,4,24,128]{4,3,2,1,0:T(8,128)}, f32[4,16,4,24,128]{4,3,2,1,0:T(8,128)S(1)}, u32[]{:S(2)}) copy-start(f32[4,16,4,24,128]{4,3,2,1,0:T(8,128)S(1)} %along_xyz.1) | copy-start | bytes 9437188

commit v3 on v2

--- a/solution.py
+++ b/solution.py
@@ -1,5 +1,6 @@
 import jax
 import jax.numpy as jnp
+import numpy as np
 from jax import lax
 from jax.experimental import pallas as pl
 from jax.experimental.pallas import tpu as pltpu
@@ -12,12 +13,10 @@
 
 
 def log_kernel(row_count, col_count, offset, radius):
-    in_index = lax.broadcasted_iota(jnp.int32, (row_count, col_count), 0)
-    out_index = lax.broadcasted_iota(jnp.int32, (row_count, col_count), 1)
-    apart = in_index - offset - out_index
-    distance = apart.astype(jnp.float32)
-    inside = jnp.abs(apart) <= radius
-    return jnp.where(inside, jnp.exp(-2.0 * distance * distance / float(radius * radius)), 0.0)
+    apart = np.arange(row_count)[:, None] - offset - np.arange(col_count)[None, :]
+    distance = apart.astype(np.float32)
+    inside = np.abs(apart) <= radius
+    return np.where(inside, np.exp(-2.0 * distance * distance / float(radius * radius)), 0.0).astype(np.float32)
 
 
 def halves(values):
@@ -27,22 +26,72 @@
 
 
 def table_halves(table):
-    high = lax.reduce_precision(table, 8, 7)
-    return high.astype(jnp.bfloat16), (table - high).astype(jnp.bfloat16)
+    high = table.astype(jnp.bfloat16)
+    return high, (table - high.astype(np.float32)).astype(jnp.bfloat16)
 
 
 def table_rows(table):
-    high, low = table_halves(table)
-    return jnp.concatenate([high, high, low], axis=0)
+    return np.concatenate(table_halves(table), axis=0)
 
 
 def table_cols(table):
     high, low = table_halves(table)
-    return jnp.concatenate([high, high, low], axis=1)
+    return np.concatenate([high, high, low], axis=1)
 
 
 def dot(left, right):
     return jnp.dot(left, right, preferred_element_type=jnp.float32)
+
+
+def proximal(logs, outer_field):
+    shifted = logs - 0.5 * outer_field
+    softer = jnp.maximum(shifted, 0.0) + jnp.log(1.0 + jnp.exp(-jnp.abs(shifted)))
+    exp_level = 1.0 + softer
+    log_level = jnp.log(exp_level)
+    log_level = log_level - (log_level + exp_level - shifted) / (1.0 + exp_level)
+    exp_level = jnp.exp(log_level)
+    log_level = log_level - (log_level + exp_level - shifted) / (1.0 + exp_level)
+    return log_level - logs, log_level
+
+
+def finish(turned, outer, at, r, out_at, dual, density):
+    for k in range(at[1] // WIDE):
+        there = pl.ds(pl.multiple_of(at[0] + k * WIDE, WIDE), WIDE)
+        put = pl.ds(pl.multiple_of(out_at + k * WIDE, WIDE), WIDE)
+        dual_part, density_part = proximal(turned(k).T, outer[r, :, there])
+        dual[r, :, put] = dual_part
+        density[r, :, put] = density_part
+
+
+def end_kernel(done_dual, done_density, rest, outer, dual, density, rest_in, outer_in, dual_in, density_in, sems):
+    depth, own_rows, length = outer.shape
+    before = done_dual.shape[-1]
+    width = length - before
+    late = [
+        pltpu.make_async_copy(rest, rest_in, sems.at[0]),
+        pltpu.make_async_copy(outer.at[:, :, pl.ds(before, width)], outer_in, sems.at[1]),
+    ]
+    for copy in late:
+        copy.start()
+    out = [
+        pltpu.make_async_copy(done_dual, dual.at[:, :, pl.ds(0, before)], sems.at[2]),
+        pltpu.make_async_copy(done_density, density.at[:, :, pl.ds(0, before)], sems.at[3]),
+    ]
+    for copy in out:
+        copy.start()
+    for copy in late:
+        copy.wait()
+    for r in range(depth):
+        def turned(k):
+            return rest_in[8 * k:8 * k + 8, :, r * ROWS:(r + 1) * ROWS, :].reshape(WIDE, LANES)
+
+        finish(turned, outer_in, (0, width), r, 0, dual_in, density_in)
+        for i, (source, target) in enumerate(((dual_in, dual), (density_in, density))):
+            copy = pltpu.make_async_copy(source.at[r], target.at[r, :, pl.ds(before, width)], sems.at[4 + 2 * r + i])
+            copy.start()
+            out.append(copy)
+    for copy in out:
+        copy.wait()
 
 
 MESH = pl.DeviceIdType.MESH
@@ -52,7 +101,35 @@
 EMPTY = -1e30
 
 
-def chain_kernel(potential, x_table, y_table, z_table, home, cells, a, b, c, d, e, f, load_sem, send_sem, recv_sem, own_sem):
+def chain_kernel(
+    potential,
+    outer,
+    x_source,
+    y_source,
+    z_source,
+    done_dual,
+    done_density,
+    rest,
+    cells,
+    a,
+    b,
+    c,
+    d,
+    e,
+    f,
+    home,
+    outer_in,
+    dual_in,
+    density_in,
+    x_table,
+    y_table,
+    z_table,
+    load_sem,
+    send_sem,
+    recv_sem,
+    own_sem,
+    out_sem,
+):
     depth, own_rows, length = potential.shape
     slab, part = lax.axis_index("gz"), lax.axis_index("gy")
     spot, lane = slab // GROUPS, slab % GROUPS
@@ -62,8 +139,22 @@
     step_x = length // CHUNKS
     tile = a.shape[2]
 
-    load = pltpu.make_async_copy(potential, cells.at[:, :, pl.ds(LANES, length)], load_sem)
-    load.start()
+    early = step_x + LANES
+    loads = [
+        pltpu.make_async_copy(potential.at[:, :, pl.ds(0, early)], cells.at[:, :, pl.ds(LANES, early)], load_sem.at[0]),
+        pltpu.make_async_copy(
+            potential.at[:, :, pl.ds(early, length - early)],
+            cells.at[:, :, pl.ds(LANES + early, length - early)],
+            load_sem.at[1],
+        ),
+        pltpu.make_async_copy(outer.at[:, :, pl.ds(0, length - step_x)], outer_in, load_sem.at[2]),
+    ]
+    tables = [
+        pltpu.make_async_copy(source, target, load_sem.at[3 + i])
+        for i, (source, target) in enumerate(((x_source, x_table), (y_source, y_table), (z_source, z_table)))
+    ]
+    for load in loads[:1] + tables + loads[1:]:
+        load.start()
 
     def z_peer(s):
         t = (s * 3) % RING
@@ -122,7 +213,7 @@
                 window = jnp.concatenate([weights[j] * jnp.exp(peaks[j] - top) for j in near], axis=1)
                 high, low = halves(window)
                 summed = (
-                    dot(high, x_table[:size, :]) + dot(low, x_table[size:2 * size, :]) + dot(high, x_table[2 * size:, :])
+                    dot(high, x_table[:size, :]) + dot(low, x_table[:size, :]) + dot(high, x_table[size:, :])
                 )
                 turned = (jnp.log(summed) + top).T
                 a[chunk, 8 * k:8 * k + 8, pl.ds(pl.multiple_of(r * 32, 32), 32), :] = turned.reshape(8, 32, LANES)
@@ -170,8 +261,8 @@
                 high, low = halves(window)
                 start = (near[0] - (k - 1)) * LANES
                 width = len(near) * LANES
-                tall = [y_table[i * size + start:i * size + start + width, :] for i in range(3)]
-                logs = jnp.log(dot(high, tall[0]) + dot(low, tall[1]) + dot(high, tall[2])) + top
+                tall = [y_table[i * size + start:i * size + start + width, :] for i in range(2)]
+                logs = jnp.log(dot(high, tall[0]) + dot(low, tall[0]) + dot(high, tall[1])) + top
                 for r in range(depth):
                     for g in range(4):
                         at = pl.multiple_of((lo * depth + r) * ROWS, ROWS)
@@ -212,24 +303,27 @@
         at = pl.multiple_of((slab_of % GROUPS) * rows, rows)
         return f.at[chunk, pl.ds(part_of * 4, 4), pl.ds(at, rows)]
 
-    def back_stage(chunk):
+    def back_stage(chunk, place):
         rows = pl.ds(pl.multiple_of(spot * tile, tile), tile)
         keep(e.at[chunk, rows], f.at[chunk, spot], 2, chunk).wait()
         arrive(2, chunk, e.at[chunk, pl.ds(0, (RING - 1) * tile)], f.at[chunk, pl.ds(0, RING - 1)]).wait_recv()
-        keep(piece(chunk, slab, part), home.at[chunk, mine], 3, chunk).start()
+        keep(piece(chunk, slab, part), place.at[mine], 3, chunk).start()
 
         @pl.loop(1, RING)
         def _(s):
             to = z_peer(s)
-            send(piece(chunk, *to), home.at[chunk, mine], 3, chunk, to)
+            send(piece(chunk, *to), place.at[mine], 3, chunk, to)
 
     edge = jnp.full((depth, own_rows, LANES), EMPTY, jnp.float32)
     cells[:, :, :LANES] = edge
     cells[:, :, LANES + length:] = edge
-    load.wait()
+    loads[0].wait()
+    tables[0].wait()
     x_stage(0)
     pl.semaphore_wait(barrier, 2 * (RING - 1))
     x_send(0)
+    for load in loads[1:2] + tables[1:]:
+        load.wait()
 
     @pl.loop(1, CHUNKS)
     def _(chunk):
@@ -242,44 +336,52 @@
 
         @pl.when(chunk > 0)
         def _():
-            back_stage(chunk - 1)
+            back_stage(chunk - 1, home.at[chunk - 1])
 
         z_stage(chunk)
 
-    back_stage(CHUNKS - 1)
+    back_stage(CHUNKS - 1, rest)
+    loads[2].wait()
+    some = pl.ds(0, RING - 1)
+
+    def out_copies(chunk):
+        at = pl.ds(pl.multiple_of(chunk * step_x, step_x), step_x)
+        return [
+            pltpu.make_async_copy(source.at[:, :, at], target.at[:, :, at], out_sem.at[i, chunk])
+            for i, (source, target) in enumerate(((dual_in, done_dual), (density_in, done_density)))
+        ]
+
+    @pl.loop(0, CHUNKS - 1)
+    def _(chunk):
+        keep(piece(chunk, slab, part), home.at[chunk, mine], 3, chunk).wait()
+        arrive(3, chunk, home.at[chunk, some], home.at[chunk, some]).wait_recv()
+
+        @pl.loop(0, depth)
+        def _(r):
+            def turned(k):
+                rows = pl.ds(pl.multiple_of(r * ROWS, ROWS), ROWS)
+                return home[chunk, 8 * k:8 * k + 8, :, rows, :].reshape(WIDE, LANES)
+
+            finish(turned, outer_in, (chunk * step_x, step_x), r, chunk * step_x, dual_in, density_in)
+
+        for copy in out_copies(chunk):
+            copy.start()
+
+    @pl.loop(0, CHUNKS - 1)
+    def _(chunk):
+        for copy in out_copies(chunk):
+            copy.wait()
 
     @pl.loop(0, CHUNKS)
     def _(chunk):
-        some = pl.ds(0, RING - 1)
         flat = pl.ds(0, (RING - 1) * tile)
         arrive(0, chunk, a.at[chunk, some], b.at[chunk, some]).wait_send()
         arrive(1, chunk, c.at[chunk, some], d.at[chunk, flat]).wait_send()
         arrive(2, chunk, e.at[chunk, flat], f.at[chunk, some]).wait_send()
-        keep(piece(chunk, slab, part), home.at[chunk, mine], 3, chunk).wait()
-        last = arrive(3, chunk, home.at[chunk, some], home.at[chunk, some])
-        last.wait_send()
-        last.wait_recv()
-
-
-def proximal(logs, outer_field):
-    shifted = logs - 0.5 * outer_field
-    softer = jnp.maximum(shifted, 0.0) + jnp.log1p(jnp.exp(-jnp.abs(shifted)))
-    log_level = jnp.log1p(softer)
-    for newton_step in range(2):
-        exp_level = jnp.exp(log_level)
-        log_level = log_level - (log_level + exp_level - shifted) / (1.0 + exp_level)
-    return log_level - logs, log_level
-
-
-def end_kernel(source, outer, dual, density):
-    blocks = outer.shape[-1] // WIDE
-    per = WIDE // ROWS
-    for k in range(blocks):
-        turned = source[k * per:(k + 1) * per].reshape(WIDE, LANES)
-        at = slice(k * WIDE, (k + 1) * WIDE)
-        dual_part, density_part = proximal(turned.T, outer[0, :, at])
-        dual[0, :, at] = dual_part
-        density[0, :, at] = density_part
+        arrive(3, chunk, rest.at[some], rest.at[some]).wait_send()
+
+    keep(piece(CHUNKS - 1, slab, part), rest.at[mine], 3, CHUNKS - 1).wait()
+    arrive(3, CHUNKS - 1, rest.at[some], rest.at[some]).wait_recv()
 
 
 def local(potential, external):
@@ -287,18 +389,22 @@
     groups = lax.axis_size("gz")
     rows = depth * ROWS
     tile = GROUPS * rows
-    vmem = pl.BlockSpec(memory_space=pltpu.VMEM)
+    wide = length // CHUNKS
+    before = length - wide
     anywhere = pl.BlockSpec(memory_space=pl.ANY)
-    x_table = table_rows(log_kernel(4 * LANES, WIDE, RADIUS, RADIUS))
-    y_table = table_rows(log_kernel(3 * LANES, LANES, RADIUS, RADIUS))
-    z_table = table_cols(log_kernel(groups * depth, groups * depth, 0, RADIUS))
+    x_table = jnp.asarray(table_rows(log_kernel(4 * LANES, WIDE, RADIUS, RADIUS)))
+    y_table = jnp.asarray(table_rows(log_kernel(3 * LANES, LANES, RADIUS, RADIUS)))
+    z_table = jnp.asarray(table_cols(log_kernel(groups * depth, groups * depth, 0, RADIUS)))
     stack = pltpu.VMEM((CHUNKS, RING, tile, LANES), jnp.float32)
     long = pltpu.VMEM((CHUNKS, RING * tile, LANES), jnp.float32)
-    along_z = pl.pallas_call(
+    done = (depth, own_rows, before)
+    done_shape = jax.ShapeDtypeStruct(done, jnp.float32)
+    piece = (RING, GROUPS, rows, LANES)
+    done_dual, done_density, rest = pl.pallas_call(
         chain_kernel,
-        out_shape=jax.ShapeDtypeStruct((CHUNKS, RING, GROUPS, rows, LANES), jnp.float32),
-        in_specs=[anywhere, vmem, vmem, vmem],
-        out_specs=anywhere,
+        out_shape=(done_shape, done_shape, jax.ShapeDtypeStruct(piece, jnp.float32)),
+        in_specs=[pl.BlockSpec(memory_space=pltpu.HBM)] * 5,
+        out_specs=(anywhere, anywhere, anywhere),
         scratch_shapes=[
             pltpu.VMEM((depth, own_rows, length + 2 * LANES), jnp.float32),
             stack,
@@ -307,25 +413,31 @@
             long,
             long,
             stack,
-            pltpu.SemaphoreType.DMA,
+            pltpu.VMEM((CHUNKS - 1,) + piece, jnp.float32),
+            pltpu.VMEM(done, jnp.float32),
+            pltpu.VMEM(done, jnp.float32),
+            pltpu.VMEM(done, jnp.float32),
+            *[pltpu.VMEM(table.shape, table.dtype) for table in (x_table, y_table, z_table)],
+            pltpu.SemaphoreType.DMA((6,)),
             pltpu.SemaphoreType.DMA((4, CHUNKS)),
             pltpu.SemaphoreType.DMA((4, CHUNKS)),
             pltpu.SemaphoreType.DMA((4, CHUNKS)),
+            pltpu.SemaphoreType.DMA((2, CHUNKS)),
         ],
-        compiler_params=pltpu.CompilerParams(collective_id=0, has_side_effects=True, vmem_limit_bytes=48 << 20),
+        compiler_params=pltpu.CompilerParams(collective_id=0, has_side_effects=True, vmem_limit_bytes=44 << 20),
         name="along_xyz",
-    )(potential, x_table, y_table, z_table)
+    )(*[pltpu.with_memory_space_constraint(v, pltpu.HBM) for v in (potential, external, x_table, y_table, z_table)])
     field = jax.ShapeDtypeStruct(potential.shape, jnp.float32)
-    wide = length // CHUNKS
-    block = pl.BlockSpec((1, own_rows, wide), lambda r, k: (r, 0, k))
+    late = pltpu.VMEM((depth, own_rows, wide), jnp.float32)
     return pl.pallas_call(
         end_kernel,
-        grid=(depth, CHUNKS),
         out_shape=(field, field),
-        in_specs=[pl.BlockSpec((wide // ROWS, ROWS, LANES), lambda r, k: (k, r, 0)), block],
-        out_specs=(block, block),
+        in_specs=[anywhere] * 3 + [pl.BlockSpec(memory_space=pltpu.HBM)],
+        out_specs=(anywhere, anywhere),
+        scratch_shapes=[pltpu.VMEM(piece, jnp.float32), late, late, late, pltpu.SemaphoreType.DMA((4 + 2 * depth,))],
+        compiler_params=pltpu.CompilerParams(vmem_limit_bytes=16 << 20),
         name="proximal",
-    )(along_z.reshape(length // ROWS, rows, LANES), external)
+    )(done_dual, done_density, rest, pltpu.with_memory_space_constraint(external, pltpu.HBM))
 
 
 def solution(mesh):

time: 164 us -> 154 us (0.939)
  Pallas kernels: 161 us -> 153 us
    pallas_call x2, Pallas kernels: 161 us -> 153 us  [the longest x1 149 us: local(): pl.pallas_call(chain_kernel, out_shape=(done_shape, done_shape, jax.Shape...]
where the time goes in v3:
time: 154 us; the launch traced here: 153 us
  Pallas kernels  153 us (99%)
    pallas_call x1, Pallas kernels, local(): pl.pallas_call(chain_kernel, out_shape=(done_shape, done_shape, jax.Shape...  149 us
    pallas_call x1, Pallas kernels, local(): pl.pallas_call(end_kernel, out_shape=(field, field), in_specs=[anywhere]...  3.46 us

profile of v3, /device:TPU:1, one launch (start us, length us, event | category | flops | bytes accessed | tf_op | source)
XLA Modules:
  0.0 153.4 jit_solution(15847169597190247004)
XLA Ops:
  0.6 149.3 %along_xyz.1 = (f32[3,128,1536]{2,1,0:T(8,128)S(1)}, f32[3,128,1536]{2,1,0:T(8,128)S(1)}, f32[16,4,24,128]{3,2,1,0:T(8,128)S(1)}) custom-call(f32[3,128,2048]{2,1,0:T(8,128)} %potential.1, f32[3,128,2048]{2,1,0:T(8,128)} %outer.3, bf16[1024,256]{1,0:T(8,128)(2,1)} %constant.6.clone.x_source, bf16[768,128]{1,0:T(8,128)(2,1)} %constant.7.clone.y_source, ...), custom_call_target="tpu_custom_call" | custom-call | tf_op jit(solution)/shard_map/along_xyz/pallas_call | solution.py:403
  150.0 3.5 %proximal.1 = (f32[3,128,2048]{2,1,0:T(8,128)}, f32[3,128,2048]{2,1,0:T(8,128)}) custom-call(f32[3,128,1536]{2,1,0:T(8,128)S(1)} %get-tuple-element.5.done_dual, f32[3,128,1536]{2,1,0:T(8,128)S(1)} %get-tuple-element.6.done_density, f32[16,4,24,128]{3,2,1,0:T(8,128)S(1)} %get-tuple-element.7.rest, f32[3,128,2048]{2,1,0:T(8,128)} %outer.3), custom_call_target="tpu_custom_call" | custom-call | tf_op jit(solution)/shard_map/proximal/pallas_call | solution.py:432

commit v4 on v3

--- a/solution.py
+++ b/solution.py
@@ -1,3 +1,5 @@
+import functools
+
 import jax
 import jax.numpy as jnp
 import numpy as np
@@ -65,31 +67,34 @@
 
 def end_kernel(done_dual, done_density, rest, outer, dual, density, rest_in, outer_in, dual_in, density_in, sems):
     depth, own_rows, length = outer.shape
-    before = done_dual.shape[-1]
-    width = length - before
+    width = outer_in.shape[-1]
+    before = length - width
+    last = pl.ds(depth - 1, 1)
     late = [
         pltpu.make_async_copy(rest, rest_in, sems.at[0]),
-        pltpu.make_async_copy(outer.at[:, :, pl.ds(before, width)], outer_in, sems.at[1]),
+        pltpu.make_async_copy(outer.at[last, :, pl.ds(before, width)], outer_in, sems.at[1]),
     ]
     for copy in late:
         copy.start()
-    out = [
-        pltpu.make_async_copy(done_dual, dual.at[:, :, pl.ds(0, before)], sems.at[2]),
-        pltpu.make_async_copy(done_density, density.at[:, :, pl.ds(0, before)], sems.at[3]),
-    ]
+    out = []
+    for i, (source, target) in enumerate(((done_dual, dual), (done_density, density))):
+        whole = pl.ds(0, depth - 1)
+        out.append(pltpu.make_async_copy(source.at[whole], target.at[whole], sems.at[2 + i]))
+        some = (last, slice(None), pl.ds(0, before))
+        out.append(pltpu.make_async_copy(source.at[some], target.at[some], sems.at[4 + i]))
     for copy in out:
         copy.start()
     for copy in late:
         copy.wait()
-    for r in range(depth):
-        def turned(k):
-            return rest_in[8 * k:8 * k + 8, :, r * ROWS:(r + 1) * ROWS, :].reshape(WIDE, LANES)
-
-        finish(turned, outer_in, (0, width), r, 0, dual_in, density_in)
-        for i, (source, target) in enumerate(((dual_in, dual), (density_in, density))):
-            copy = pltpu.make_async_copy(source.at[r], target.at[r, :, pl.ds(before, width)], sems.at[4 + 2 * r + i])
-            copy.start()
-            out.append(copy)
+
+    def turned(k):
+        return rest_in[8 * k:8 * k + 8].reshape(WIDE, LANES)
+
+    finish(turned, outer_in, (0, width), 0, 0, dual_in, density_in)
+    for i, (source, target) in enumerate(((dual_in, dual), (density_in, density))):
+        copy = pltpu.make_async_copy(source, target.at[last, :, pl.ds(before, width)], sems.at[6 + i])
+        copy.start()
+        out.append(copy)
     for copy in out:
         copy.wait()
 
@@ -147,7 +152,7 @@
             cells.at[:, :, pl.ds(LANES + early, length - early)],
             load_sem.at[1],
         ),
-        pltpu.make_async_copy(outer.at[:, :, pl.ds(0, length - step_x)], outer_in, load_sem.at[2]),
+        pltpu.make_async_copy(outer, outer_in, load_sem.at[2]),
     ]
     tables = [
         pltpu.make_async_copy(source, target, load_sem.at[3 + i])
@@ -157,9 +162,10 @@
         load.start()
 
     def z_peer(s):
-        t = (s * 3) % RING
-        to_level = (level + sign * (t % 8) + 8) % 8
-        to_core = (core + t // 8) % 2
+        k = (s - 1) // 2
+        away = 4 + (1 - 2 * (k % 2)) * ((k + 1) // 2)
+        to_level = (level + sign * away + 8) % 8
+        to_core = (core + s % 2) % 2
         return spot * GROUPS + to_level % 4, (to_level // 4) * 2 + to_core
 
     def xy_peer(s):
@@ -194,39 +200,35 @@
     def keep(source, target, stage, chunk):
         return pltpu.make_async_copy(source, target, own_sem.at[stage, chunk])
 
-    def x_stage(chunk):
-        @pl.loop(0, depth)
-        def _(r):
-            peaks, weights = [], []
-            for k in range(6):
-                at = pl.multiple_of(chunk * step_x + k * LANES, LANES)
-                block = cells[r, :, pl.ds(at, LANES)]
-                peak = jnp.max(block, axis=1, keepdims=True)
-                peaks.append(peak)
-                weights.append(jnp.exp(block - peak))
-            size = 4 * LANES
-            for k in range(2):
-                near = range(2 * k, 2 * k + 4)
-                top = peaks[near[0]]
-                for j in near[1:]:
-                    top = jnp.maximum(top, peaks[j])
-                window = jnp.concatenate([weights[j] * jnp.exp(peaks[j] - top) for j in near], axis=1)
-                high, low = halves(window)
-                summed = (
-                    dot(high, x_table[:size, :]) + dot(low, x_table[:size, :]) + dot(high, x_table[size:, :])
-                )
-                turned = (jnp.log(summed) + top).T
-                a[chunk, 8 * k:8 * k + 8, pl.ds(pl.multiple_of(r * 32, 32), 32), :] = turned.reshape(8, 32, LANES)
-
-        return None
-
-    def x_send(chunk):
-        keep(a.at[chunk, mine], b.at[chunk, slot], 0, chunk).start()
+    def x_row(chunk, r):
+        peaks, weights = [], []
+        for k in range(6):
+            at = pl.multiple_of(chunk * step_x + k * LANES, LANES)
+            block = cells[r, :, pl.ds(at, LANES)]
+            peak = jnp.max(block, axis=1, keepdims=True)
+            peaks.append(peak)
+            weights.append(jnp.exp(block - peak))
+        size = 4 * LANES
+        for k in range(2):
+            near = range(2 * k, 2 * k + 4)
+            top = peaks[near[0]]
+            for j in near[1:]:
+                top = jnp.maximum(top, peaks[j])
+            window = jnp.concatenate([weights[j] * jnp.exp(peaks[j] - top) for j in near], axis=1)
+            high, low = halves(window)
+            summed = (
+                dot(high, x_table[:size, :]) + dot(low, x_table[:size, :]) + dot(high, x_table[size:, :])
+            )
+            turned = (jnp.log(summed) + top).T
+            a[chunk, 8 * k:8 * k + 8, pl.ds(pl.multiple_of(r * 32, 32), 32), :] = turned.reshape(8, 32, LANES)
+
+    def x_send(chunk, r=None):
+        rows = pl.ds(0, tile) if r is None else pl.ds(r * 32, 32)
 
         @pl.loop(1, RING)
         def _(s):
             to = z_peer(s)
-            send(a.at[chunk, order(*to)], b.at[chunk, slot], 0, chunk, to)
+            send(a.at[chunk, order(*to), rows], b.at[chunk, slot, rows], 0, chunk, to)
 
     def arrive(stage, chunk, source, target):
         view = pltpu.make_async_remote_copy(
@@ -303,31 +305,55 @@
         at = pl.multiple_of((slab_of % GROUPS) * rows, rows)
         return f.at[chunk, pl.ds(part_of * 4, 4), pl.ds(at, rows)]
 
-    def back_stage(chunk, place):
+    def back_wait(chunk):
         rows = pl.ds(pl.multiple_of(spot * tile, tile), tile)
         keep(e.at[chunk, rows], f.at[chunk, spot], 2, chunk).wait()
         arrive(2, chunk, e.at[chunk, pl.ds(0, (RING - 1) * tile)], f.at[chunk, pl.ds(0, RING - 1)]).wait_recv()
-        keep(piece(chunk, slab, part), place.at[mine], 3, chunk).start()
+
+    def back_send(source, target, stage, column):
+        keep(source(slab, part), target, stage, column).start()
 
         @pl.loop(1, RING)
         def _(s):
             to = z_peer(s)
-            send(piece(chunk, *to), place.at[mine], 3, chunk, to)
+            send(source(*to), target, stage, column, to)
+
+    def back_stage(chunk):
+        back_wait(chunk)
+        back_send(functools.partial(piece, chunk), home.at[chunk, mine], 3, chunk)
+
+    final = CHUNKS - 1
+
+    def row_piece(r, slab_of, part_of):
+        at = pl.multiple_of((slab_of % GROUPS) * (tile // GROUPS) + r * ROWS, ROWS)
+        return f.at[final, pl.ds(part_of * 4, 4), pl.ds(at, ROWS)]
+
+    def row_place(r, which):
+        return rest.at[which] if r == depth - 1 else home.at[final, which, :, pl.ds(r * ROWS, ROWS)]
+
+    row_sems = [(3, final)] + [(4, r - 1) for r in range(1, depth)]
 
     edge = jnp.full((depth, own_rows, LANES), EMPTY, jnp.float32)
     cells[:, :, :LANES] = edge
     cells[:, :, LANES + length:] = edge
     loads[0].wait()
     tables[0].wait()
-    x_stage(0)
-    pl.semaphore_wait(barrier, 2 * (RING - 1))
-    x_send(0)
+    for r in range(depth):
+        x_row(0, r)
+        if r == 0:
+            pl.semaphore_wait(barrier, 2 * (RING - 1))
+        x_send(0, r)
+    keep(a.at[0, mine], b.at[0, slot], 0, 0).start()
     for load in loads[1:2] + tables[1:]:
         load.wait()
 
     @pl.loop(1, CHUNKS)
     def _(chunk):
-        x_stage(chunk)
+        @pl.loop(0, depth)
+        def _(r):
+            x_row(chunk, r)
+
+        keep(a.at[chunk, mine], b.at[chunk, slot], 0, chunk).start()
         x_send(chunk)
 
     @pl.loop(0, CHUNKS)
@@ -336,40 +362,60 @@
 
         @pl.when(chunk > 0)
         def _():
-            back_stage(chunk - 1, home.at[chunk - 1])
+            back_stage(chunk - 1)
 
         z_stage(chunk)
 
-    back_stage(CHUNKS - 1, rest)
+    back_wait(final)
+    for r in range(depth):
+        back_send(functools.partial(row_piece, r), row_place(r, mine), *row_sems[r])
     loads[2].wait()
     some = pl.ds(0, RING - 1)
 
-    def out_copies(chunk):
+    def out_copies(rows, chunk, column):
         at = pl.ds(pl.multiple_of(chunk * step_x, step_x), step_x)
         return [
-            pltpu.make_async_copy(source.at[:, :, at], target.at[:, :, at], out_sem.at[i, chunk])
+            pltpu.make_async_copy(source.at[rows, :, at], target.at[rows, :, at], out_sem.at[i, column])
             for i, (source, target) in enumerate(((dual_in, done_dual), (density_in, done_density)))
         ]
 
-    @pl.loop(0, CHUNKS - 1)
+    every = pl.ds(0, depth)
+
+    def row(chunk, r):
+        def turned(k):
+            rows = pl.ds(pl.multiple_of(r * ROWS, ROWS), ROWS)
+            return home[chunk, 8 * k:8 * k + 8, :, rows, :].reshape(WIDE, LANES)
+
+        finish(turned, outer_in, (chunk * step_x, step_x), r, chunk * step_x, dual_in, density_in)
+
+    @pl.loop(0, final)
     def _(chunk):
         keep(piece(chunk, slab, part), home.at[chunk, mine], 3, chunk).wait()
         arrive(3, chunk, home.at[chunk, some], home.at[chunk, some]).wait_recv()
 
         @pl.loop(0, depth)
         def _(r):
-            def turned(k):
-                rows = pl.ds(pl.multiple_of(r * ROWS, ROWS), ROWS)
-                return home[chunk, 8 * k:8 * k + 8, :, rows, :].reshape(WIDE, LANES)
-
-            finish(turned, outer_in, (chunk * step_x, step_x), r, chunk * step_x, dual_in, density_in)
-
-        for copy in out_copies(chunk):
+            row(chunk, r)
+
+        for copy in out_copies(every, chunk, chunk):
             copy.start()
 
-    @pl.loop(0, CHUNKS - 1)
-    def _(chunk):
-        for copy in out_copies(chunk):
+    for r in range(depth):
+        keep(row_piece(r, slab, part), row_place(r, mine), *row_sems[r]).wait()
+        if r == depth - 1:
+            break
+        arrive(*row_sems[r], row_place(r, some), row_place(r, some)).wait_recv()
+        row(final, r)
+        for copy in out_copies(pl.ds(r, 1), final, final + r):
+            copy.start()
+
+    @pl.loop(0, final)
+    def _(chunk):
+        for copy in out_copies(every, chunk, chunk):
+            copy.wait()
+
+    for r in range(depth - 1):
+        for copy in out_copies(pl.ds(r, 1), final, final + r):
             copy.wait()
 
     @pl.loop(0, CHUNKS)
@@ -378,10 +424,14 @@
         arrive(0, chunk, a.at[chunk, some], b.at[chunk, some]).wait_send()
         arrive(1, chunk, c.at[chunk, some], d.at[chunk, flat]).wait_send()
         arrive(2, chunk, e.at[chunk, flat], f.at[chunk, some]).wait_send()
-        arrive(3, chunk, rest.at[some], rest.at[some]).wait_send()
-
-    keep(piece(CHUNKS - 1, slab, part), rest.at[mine], 3, CHUNKS - 1).wait()
-    arrive(3, CHUNKS - 1, rest.at[some], rest.at[some]).wait_recv()
+
+    @pl.loop(0, final)
+    def _(chunk):
+        arrive(3, chunk, home.at[chunk, some], home.at[chunk, some]).wait_send()
+
+    for r in range(depth):
+        arrive(*row_sems[r], row_place(r, some), row_place(r, some)).wait_send()
+    arrive(*row_sems[-1], row_place(depth - 1, some), row_place(depth - 1, some)).wait_recv()
 
 
 def local(potential, external):
@@ -390,19 +440,18 @@
     rows = depth * ROWS
     tile = GROUPS * rows
     wide = length // CHUNKS
-    before = length - wide
     anywhere = pl.BlockSpec(memory_space=pl.ANY)
     x_table = jnp.asarray(table_rows(log_kernel(4 * LANES, WIDE, RADIUS, RADIUS)))
     y_table = jnp.asarray(table_rows(log_kernel(3 * LANES, LANES, RADIUS, RADIUS)))
     z_table = jnp.asarray(table_cols(log_kernel(groups * depth, groups * depth, 0, RADIUS)))
     stack = pltpu.VMEM((CHUNKS, RING, tile, LANES), jnp.float32)
     long = pltpu.VMEM((CHUNKS, RING * tile, LANES), jnp.float32)
-    done = (depth, own_rows, before)
-    done_shape = jax.ShapeDtypeStruct(done, jnp.float32)
-    piece = (RING, GROUPS, rows, LANES)
+    field = jax.ShapeDtypeStruct(potential.shape, jnp.float32)
+    held = pltpu.VMEM(potential.shape, jnp.float32)
+    piece = (RING, GROUPS, ROWS, LANES)
     done_dual, done_density, rest = pl.pallas_call(
         chain_kernel,
-        out_shape=(done_shape, done_shape, jax.ShapeDtypeStruct(piece, jnp.float32)),
+        out_shape=(field, field, jax.ShapeDtypeStruct(piece, jnp.float32)),
         in_specs=[pl.BlockSpec(memory_space=pltpu.HBM)] * 5,
         out_specs=(anywhere, anywhere, anywhere),
         scratch_shapes=[
@@ -413,28 +462,27 @@
             long,
             long,
             stack,
-            pltpu.VMEM((CHUNKS - 1,) + piece, jnp.float32),
-            pltpu.VMEM(done, jnp.float32),
-            pltpu.VMEM(done, jnp.float32),
-            pltpu.VMEM(done, jnp.float32),
+            pltpu.VMEM((CHUNKS, RING, GROUPS, rows, LANES), jnp.float32),
+            held,
+            held,
+            held,
             *[pltpu.VMEM(table.shape, table.dtype) for table in (x_table, y_table, z_table)],
             pltpu.SemaphoreType.DMA((6,)),
-            pltpu.SemaphoreType.DMA((4, CHUNKS)),
-            pltpu.SemaphoreType.DMA((4, CHUNKS)),
-            pltpu.SemaphoreType.DMA((4, CHUNKS)),
-            pltpu.SemaphoreType.DMA((2, CHUNKS)),
+            pltpu.SemaphoreType.DMA((5, CHUNKS)),
+            pltpu.SemaphoreType.DMA((5, CHUNKS)),
+            pltpu.SemaphoreType.DMA((5, CHUNKS)),
+            pltpu.SemaphoreType.DMA((2, CHUNKS - 1 + depth)),
         ],
         compiler_params=pltpu.CompilerParams(collective_id=0, has_side_effects=True, vmem_limit_bytes=44 << 20),
         name="along_xyz",
     )(*[pltpu.with_memory_space_constraint(v, pltpu.HBM) for v in (potential, external, x_table, y_table, z_table)])
-    field = jax.ShapeDtypeStruct(potential.shape, jnp.float32)
-    late = pltpu.VMEM((depth, own_rows, wide), jnp.float32)
+    late = pltpu.VMEM((1, own_rows, wide), jnp.float32)
     return pl.pallas_call(
         end_kernel,
         out_shape=(field, field),
         in_specs=[anywhere] * 3 + [pl.BlockSpec(memory_space=pltpu.HBM)],
         out_specs=(anywhere, anywhere),
-        scratch_shapes=[pltpu.VMEM(piece, jnp.float32), late, late, late, pltpu.SemaphoreType.DMA((4 + 2 * depth,))],
+        scratch_shapes=[pltpu.VMEM(piece, jnp.float32), late, late, late, pltpu.SemaphoreType.DMA((8,))],
         compiler_params=pltpu.CompilerParams(vmem_limit_bytes=16 << 20),
         name="proximal",
     )(done_dual, done_density, rest, pltpu.with_memory_space_constraint(external, pltpu.HBM))

time: 154 us -> 153 us (level)
  no operation moved by 1% of the time
where the time goes in v4:
time: 153 us
  Pallas kernels  152 us (99%)
    pallas_call x1, Pallas kernels, local(): pl.pallas_call(chain_kernel, out_shape=(field, field, jax.ShapeDtypeStruc...  149 us

profile of v4, /device:TPU:1, one launch (start us, length us, event | category | flops | bytes accessed | tf_op | source)
XLA Modules:
  0.0 152.7 jit_solution(9007060941696825791)
XLA Ops:
  0.6 149.3 %along_xyz.1 = (f32[3,128,2048]{2,1,0:T(8,128)S(1)}, f32[3,128,2048]{2,1,0:T(8,128)S(1)}, f32[16,4,8,128]{3,2,1,0:T(8,128)S(1)}) custom-call(f32[3,128,2048]{2,1,0:T(8,128)} %potential.1, f32[3,128,2048]{2,1,0:T(8,128)} %outer.3, bf16[1024,256]{1,0:T(8,128)(2,1)} %constant.6.clone.x_source, bf16[768,128]{1,0:T(8,128)(2,1)} %constant.7.clone.y_source, ...), custom_call_target="tpu_custom_call" | custom-call | tf_op jit(solution)/shard_map/along_xyz/pallas_call | solution.py:452
  150.0 2.7 %proximal.1 = (f32[3,128,2048]{2,1,0:T(8,128)}, f32[3,128,2048]{2,1,0:T(8,128)}) custom-call(f32[3,128,2048]{2,1,0:T(8,128)S(1)} %get-tuple-element.5.done_dual, f32[3,128,2048]{2,1,0:T(8,128)S(1)} %get-tuple-element.6.done_density, f32[16,4,8,128]{3,2,1,0:T(8,128)S(1)} %get-tuple-element.7.rest, f32[3,128,2048]{2,1,0:T(8,128)} %outer.3), custom_call_target="tpu_custom_call" | custom-call | tf_op jit(solution)/shard_map/proximal/pallas_call | solution.py:480

commit v5 on v4

--- a/solution.py
+++ b/solution.py
@@ -134,6 +134,8 @@
     recv_sem,
     own_sem,
     out_sem,
+    z_ready,
+    xy_ready,
 ):
     depth, own_rows, length = potential.shape
     slab, part = lax.axis_index("gz"), lax.axis_index("gy")
@@ -176,10 +178,42 @@
 
     barrier = pltpu.get_barrier_semaphore()
 
+    first, second = (slab, part - core), (slab, part - core + 1)
+
+    @pl.loop(1, 8)
+    def _(s):
+        to_level = (level + s) % 8
+        to = spot * GROUPS + to_level % 4, (to_level // 4) * 2
+        pl.semaphore_signal(barrier, inc=1, device_id=to, device_id_type=MESH)
+
+    @pl.when(core == 1)
+    def _():
+        pl.semaphore_signal(barrier, inc=1, device_id=first, device_id_type=MESH)
+
     @pl.loop(1, RING)
     def _(s):
-        pl.semaphore_signal(barrier, inc=1, device_id=z_peer(s), device_id_type=MESH)
-        pl.semaphore_signal(barrier, inc=1, device_id=(xy_peer(s) * GROUPS + lane, part), device_id_type=MESH)
+        to = xy_peer(s) * GROUPS + lane, part - core + 1
+        pl.semaphore_signal(barrier, inc=1, device_id=to, device_id_type=MESH)
+
+    def meet_z():
+        @pl.when(core == 0)
+        def _():
+            pl.semaphore_wait(barrier, RING - 1)
+            pl.semaphore_signal(z_ready, inc=1, device_id=second, device_id_type=MESH)
+
+        @pl.when(core == 1)
+        def _():
+            pl.semaphore_wait(z_ready, 1)
+
+    def meet_xy():
+        @pl.when(core == 1)
+        def _():
+            pl.semaphore_wait(barrier, 2 * (RING - 1))
+            pl.semaphore_signal(xy_ready, inc=1, device_id=first, device_id_type=MESH)
+
+        @pl.when(core == 0)
+        def _():
+            pl.semaphore_wait(xy_ready, 1)
 
     def order(slab_of, part_of):
         return ((part_of // 2) * 4 + slab_of % GROUPS) * 2 + part_of % 2
@@ -341,7 +375,7 @@
     for r in range(depth):
         x_row(0, r)
         if r == 0:
-            pl.semaphore_wait(barrier, 2 * (RING - 1))
+            meet_z()
         x_send(0, r)
     keep(a.at[0, mine], b.at[0, slot], 0, 0).start()
     for load in loads[1:2] + tables[1:]:
@@ -355,6 +389,8 @@
 
         keep(a.at[chunk, mine], b.at[chunk, slot], 0, chunk).start()
         x_send(chunk)
+
+    meet_xy()
 
     @pl.loop(0, CHUNKS)
     def _(chunk):
@@ -472,6 +508,8 @@
             pltpu.SemaphoreType.DMA((5, CHUNKS)),
             pltpu.SemaphoreType.DMA((5, CHUNKS)),
             pltpu.SemaphoreType.DMA((2, CHUNKS - 1 + depth)),
+            pltpu.SemaphoreType.REGULAR,
+            pltpu.SemaphoreType.REGULAR,
         ],
         compiler_params=pltpu.CompilerParams(collective_id=0, has_side_effects=True, vmem_limit_bytes=44 << 20),
         name="along_xyz",

time: 153 us -> 150 us (0.980)
  Pallas kernels: 152 us -> 149 us
    pallas_call x1, Pallas kernels: 149 us -> 146 us  [local(): pl.pallas_call(chain_kernel, out_shape=(field, field, jax.ShapeDtypeStruc...]
where the time goes in v5:
time: 150 us
  Pallas kernels  149 us (99%)
    pallas_call x1, Pallas kernels, local(): pl.pallas_call(chain_kernel, out_shape=(field, field, jax.ShapeDtypeStruc...  146 us

profile of v5, /device:TPU:1, one launch (start us, length us, event | category | flops | bytes accessed | tf_op | source)
XLA Modules:
  0.0 149.6 jit_solution(8429740782231092964)
XLA Ops:
  0.6 146.2 %along_xyz.1 = (f32[3,128,2048]{2,1,0:T(8,128)S(1)}, f32[3,128,2048]{2,1,0:T(8,128)S(1)}, f32[16,4,8,128]{3,2,1,0:T(8,128)S(1)}) custom-call(f32[3,128,2048]{2,1,0:T(8,128)} %potential.1, f32[3,128,2048]{2,1,0:T(8,128)} %outer.3, bf16[1024,256]{1,0:T(8,128)(2,1)} %constant.6.clone.x_source, bf16[768,128]{1,0:T(8,128)(2,1)} %constant.7.clone.y_source, ...), custom_call_target="tpu_custom_call" | custom-call | tf_op jit(solution)/shard_map/along_xyz/pallas_call | solution.py:488
  146.8 2.7 %proximal.1 = (f32[3,128,2048]{2,1,0:T(8,128)}, f32[3,128,2048]{2,1,0:T(8,128)}) custom-call(f32[3,128,2048]{2,1,0:T(8,128)S(1)} %get-tuple-element.5.done_dual, f32[3,128,2048]{2,1,0:T(8,128)S(1)} %get-tuple-element.6.done_density, f32[16,4,8,128]{3,2,1,0:T(8,128)S(1)} %get-tuple-element.7.rest, f32[3,128,2048]{2,1,0:T(8,128)} %outer.3), custom_call_target="tpu_custom_call" | custom-call | tf_op jit(solution)/shard_map/proximal/pallas_call | solution.py:518

commit v6 on v5

--- a/solution.py
+++ b/solution.py
@@ -66,13 +66,13 @@
 
 
 def end_kernel(done_dual, done_density, rest, outer, dual, density, rest_in, outer_in, dual_in, density_in, sems):
-    depth, own_rows, length = outer.shape
+    depth, own_rows, length = dual.shape
     width = outer_in.shape[-1]
     before = length - width
     last = pl.ds(depth - 1, 1)
     late = [
         pltpu.make_async_copy(rest, rest_in, sems.at[0]),
-        pltpu.make_async_copy(outer.at[last, :, pl.ds(before, width)], outer_in, sems.at[1]),
+        pltpu.make_async_copy(outer, outer_in, sems.at[1]),
     ]
     for copy in late:
         copy.start()
@@ -115,6 +115,7 @@
     done_dual,
     done_density,
     rest,
+    rest_outer,
     cells,
     a,
     b,
@@ -406,6 +407,11 @@
     for r in range(depth):
         back_send(functools.partial(row_piece, r), row_place(r, mine), *row_sems[r])
     loads[2].wait()
+    pass_on = pltpu.make_async_copy(
+        outer_in.at[pl.ds(depth - 1, 1), :, pl.ds(length - step_x, step_x)], rest_outer, load_sem.at[2]
+    )
+    pass_on.start()
+    pass_on.wait()
     some = pl.ds(0, RING - 1)
 
     def out_copies(rows, chunk, column):
@@ -485,11 +491,16 @@
     field = jax.ShapeDtypeStruct(potential.shape, jnp.float32)
     held = pltpu.VMEM(potential.shape, jnp.float32)
     piece = (RING, GROUPS, ROWS, LANES)
-    done_dual, done_density, rest = pl.pallas_call(
+    done_dual, done_density, rest, rest_outer = pl.pallas_call(
         chain_kernel,
-        out_shape=(field, field, jax.ShapeDtypeStruct(piece, jnp.float32)),
+        out_shape=(
+            field,
+            field,
+            jax.ShapeDtypeStruct(piece, jnp.float32),
+            jax.ShapeDtypeStruct((1, own_rows, wide), jnp.float32),
+        ),
         in_specs=[pl.BlockSpec(memory_space=pltpu.HBM)] * 5,
-        out_specs=(anywhere, anywhere, anywhere),
+        out_specs=(anywhere,) * 4,
         scratch_shapes=[
             pltpu.VMEM((depth, own_rows, length + 2 * LANES), jnp.float32),
             stack,
@@ -518,12 +529,12 @@
     return pl.pallas_call(
         end_kernel,
         out_shape=(field, field),
-        in_specs=[anywhere] * 3 + [pl.BlockSpec(memory_space=pltpu.HBM)],
+        in_specs=[anywhere] * 4,
         out_specs=(anywhere, anywhere),
         scratch_shapes=[pltpu.VMEM(piece, jnp.float32), late, late, late, pltpu.SemaphoreType.DMA((8,))],
         compiler_params=pltpu.CompilerParams(vmem_limit_bytes=16 << 20),
         name="proximal",
-    )(done_dual, done_density, rest, pltpu.with_memory_space_constraint(external, pltpu.HBM))
+    )(done_dual, done_density, rest, rest_outer)
 
 
 def solution(mesh):

time: 150 us -> 150 us (level)
  no operation moved by 1% of the time
where the time goes in v6:
time: 150 us
  Pallas kernels  149 us (99%)
    pallas_call x1, Pallas kernels, local(): pl.pallas_call(chain_kernel, out_shape=(field, field, jax.ShapeDtypeStruc...  146 us

profile of v6, /device:TPU:1, one launch (start us, length us, event | category | flops | bytes accessed | tf_op | source)
XLA Modules:
  0.0 149.6 jit_solution(10485862009797644224)
XLA Ops:
  0.6 146.2 %along_xyz.1 = (f32[3,128,2048]{2,1,0:T(8,128)S(1)}, f32[3,128,2048]{2,1,0:T(8,128)S(1)}, f32[16,4,8,128]{3,2,1,0:T(8,128)S(1)}, f32[1,128,512]{2,1,0:T(8,128)S(1)}) custom-call(f32[3,128,2048]{2,1,0:T(8,128)} %potential.1, f32[3,128,2048]{2,1,0:T(8,128)} %outer.1, bf16[1024,256]{1,0:T(8,128)(2,1)} %constant.6.clone.x_source, ...), custom_call_target="tpu_custom_call" | custom-call | tf_op jit(solution)/shard_map/along_xyz/pallas_call | solution.py:494
  146.8 2.8 %proximal.1 = (f32[3,128,2048]{2,1,0:T(8,128)}, f32[3,128,2048]{2,1,0:T(8,128)}) custom-call(f32[3,128,2048]{2,1,0:T(8,128)S(1)} %get-tuple-element.6.done_dual, f32[3,128,2048]{2,1,0:T(8,128)S(1)} %get-tuple-element.7.done_density, f32[16,4,8,128]{3,2,1,0:T(8,128)S(1)} %get-tuple-element.8.rest, f32[1,128,512]{2,1,0:T(8,128)S(1)} %get-tuple-element.9.outer), custom_call_target="tpu_custom_call" | custom-call | tf_op jit(solution)/shard_map/proximal/pallas_call | solution.py:529
